TPU v7x, 128 devices: a whole 4x4x4 slice. The times are simulated.
128 devices in a mesh: hist: 8 (over x, core), tsec: 16 (over z, y).
Axes of the slice: x: 4, y: 4, z: 4, core: 2. Of those that a mesh axis runs over, the one named last changes fastest.
Arguments:
- hist_green: bfloat16 [2, 16384, 16384], P(None, 'hist', 'tsec'), may hold values from -6 to 6
- sigma_panel: bfloat16 [16384, 512], P('hist'), may hold values from -0.03125 to 0.03125
- step_operator: float32 [2, 2, 256, 256], replicated, as said below
- coupling: float32 [8, 1024], replicated, may hold values from -0.01953125 to 0.01953125
- pair_index: int32 [3, 8, 1024], replicated, may hold values from 0 to 1023
Outputs:
- new_rows: float32 [2, 16, 1024, 512], P(None, 'tsec', 'hist')
- new_sigma: bfloat16 [2, 16, 1024, 512], P(None, 'tsec', 'hist')
Inputs may be any that keep to these rules, and one draw needn't show every extreme that they name: `step_operator`: for each block the real part is symmetric and the imaginary part antisymmetric; the diagonal of the real part exceeds the sum of magnitudes of the rest of its row in the real form, so the operator is Hermitian positive definite.
All inputs are finite; a program needn't handle non-finite values.
Results may differ from a plain program's by a relative error of at most 0.0058.
Values may be sent and summed in bfloat16 or wider, within the bound.
A program may use at most 128 MiB of HBM per device.

v0:
```python
import jax
import jax.numpy as jnp
from jax import lax
from jax.sharding import PartitionSpec as P

N = 32
B = 8
NBLK = 2


def broadcast(block, axis, holder):
    block = jnp.where(lax.axis_index(axis) == holder, block, jnp.zeros_like(block))
    return lax.psum(block, axis)


def turned_panel(panel, half_width):
    return jnp.concatenate([-panel[:, half_width:], panel[:, :half_width]], axis=1)


def memory_term(green_real, green_imag, panel, turned):
    first_term = jnp.einsum("kc,kr->cr", green_real, panel, preferred_element_type=jnp.float32)
    return first_term + jnp.einsum(
        "kc,kr->cr", green_imag, turned, preferred_element_type=jnp.float32
    )


def block_solve(operator, rhs_rows):
    real_part = operator[0]
    imag_part = operator[1]
    upper_half = jnp.concatenate([real_part, -imag_part], axis=1)
    lower_half = jnp.concatenate([imag_part, real_part], axis=1)
    factor = jnp.linalg.cholesky(jnp.concatenate([upper_half, lower_half], axis=0))
    return jax.scipy.linalg.cho_solve((factor, True), rhs_rows.T).T


def self_energy(row_block, pair_index, coupling, orbit, times):
    slots = row_block.shape[0] // orbit
    field = row_block.reshape(slots, orbit, 2, times, orbit).transpose(4, 1, 2, 3, 0)
    field = field.reshape(orbit * orbit, 2, times * slots)
    term_count = pair_index.shape[1]

    def select_pairs(which):
        taken = jnp.take(field, pair_index[which].reshape(-1), axis=0)
        return taken.reshape(term_count, orbit * orbit, 2, times * slots)

    first_term = select_pairs(0)
    second_term = select_pairs(1)
    third_term = select_pairs(2)
    prod_real = (
        first_term[:, :, 0] * second_term[:, :, 0] - first_term[:, :, 1] * second_term[:, :, 1]
    )
    prod_imag = (
        first_term[:, :, 0] * second_term[:, :, 1] + first_term[:, :, 1] * second_term[:, :, 0]
    )
    trip_real = prod_real * third_term[:, :, 0] + prod_imag * third_term[:, :, 1]
    trip_imag = prod_imag * third_term[:, :, 0] - prod_real * third_term[:, :, 1]
    weights = coupling[:, :, None]
    sig_real = jnp.sum(trip_real * weights, axis=0)
    sig_imag = jnp.sum(trip_imag * weights, axis=0)
    stacked = jnp.stack([sig_real, sig_imag], axis=1).reshape(orbit, orbit, 2, times, slots)
    stacked = stacked.transpose(4, 1, 2, 3, 0).reshape(slots * orbit, 2 * times * orbit)
    return stacked.astype(jnp.bfloat16)


def per_device(hist_green, sigma_panel, step_operator, coupling, pair_index):
    hist_count = lax.axis_size("hist")
    hist_place = lax.axis_index("hist")
    column_total = hist_green.shape[2]
    column_share = column_total // hist_count
    panel_rows = hist_green.shape[1]
    half_width = sigma_panel.shape[1] // 2
    own_tail = hist_green[:, panel_rows - half_width :, :]
    tail_rows = broadcast(own_tail, "hist", hist_count - 1)
    tail_share = lax.dynamic_slice_in_dim(tail_rows, hist_place * column_share, column_share, 2)
    previous = (
        tail_share.astype(jnp.float32).transpose(2, 0, 1).reshape(column_share, 2 * half_width)
    )
    tail_term = jnp.zeros((column_total, 2 * half_width), jnp.float32)
    panel = sigma_panel
    solved_list = []
    sigma_list = []
    for block_index in range(NBLK):
        turned = turned_panel(panel, half_width)
        extra_term = tail_term if block_index == 0 else None

        def term_rows(row_start, row_count, panel=panel, turned=turned, extra_term=extra_term):
            green_real = hist_green[0]
            green_imag = hist_green[1]
            partial_rows = memory_term(green_real, green_imag, panel, turned)
            return partial_rows

        memory_all = lax.psum(term_rows(0, column_total), "hist")
        memory = lax.dynamic_slice_in_dim(memory_all, hist_place * column_share, column_share, 0)
        solution = block_solve(step_operator[block_index], previous + memory)
        sigma_new = self_energy(solution, pair_index, coupling, N, B)
        solved_list.append(solution)
        sigma_list.append(sigma_new)
        previous = solution
        if block_index + 1 < NBLK:
            column_rows = lax.all_gather(sigma_new, "hist", axis=0, tiled=True)
            every_row = lax.all_gather(column_rows, "tsec", axis=0, tiled=True)
            panel = lax.dynamic_slice_in_dim(every_row, hist_place * panel_rows, panel_rows, 0)
    return (jnp.stack(solved_list)[:, None], jnp.stack(sigma_list)[:, None])


def solution(mesh):
    return jax.shard_map(
        per_device,
        mesh=mesh,
        in_specs=(P(None, "hist", "tsec"), P("hist", None), P(), P(), P()),
        out_specs=(P(None, "tsec", "hist", None), P(None, "tsec", "hist", None)),
        check_vma=False,
    )
```

profile of v0, /device:TPU:1, one launch (start us, length us, event | category | flops | bytes accessed | tf_op | source)
XLA Modules:
  0.0 989.6 jit_solution(10898650405290552949)
XLA Ops:
  7.2 2.4 slice_select_fusion
  9.9 4.7 fusion.10
  14.7 3.7 bitcast_add_fusion
  21.0 1.4 fusion.32
  22.4 11.7 %cholesky.286 = f32[128,128]{1,0:T(8,128)S(1)} custom-call(f32[128,128]{1,0:T(8,128)S(1)} %cholesky.426), custom_call_target="Cholesky" | custom-call | tf_op jit(solution)/shard_map/jit(cholesky)/cholesky | solution.py:32
  34.2 9.8 custom-call.29
  44.8 11.7 %cholesky.305 = f32[128,128]{1,0:T(8,128)S(1)} custom-call(f32[128,128]{1,0:T(8,128)S(1)} %cholesky.430), custom_call_target="Cholesky" | custom-call | tf_op jit(solution)/shard_map/jit(cholesky)/cholesky | solution.py:32
  56.5 10.3 %custom-call.30 = f32[1,128,128]{1,2,0:T(8,128)S(1)} custom-call(f32[1,128,128]{2,1,0:T(8,128)S(1)} %get-tuple-element.92), custom_call_target="InvertDiagBlocksLowerTriangular" | custom-call | tf_op jit(solution)/shard_map/jit(cholesky)/cholesky | solution.py:32
  67.5 11.7 %cholesky.326 = f32[128,128]{1,0:T(8,128)S(1)} custom-call(f32[128,128]{1,0:T(8,128)S(1)} %cholesky.435), custom_call_target="Cholesky" | custom-call | tf_op jit(solution)/shard_map/jit(cholesky)/cholesky | solution.py:32
  79.9 9.8 custom-call.31
  90.3 11.9 %cholesky.343 = f32[128,128]{1,0:T(8,128)S(1)} custom-call(f32[128,128]{1,0:T(8,128)S(1)} %convolution_subtract_fusion.17), custom_call_target="Cholesky" | custom-call | tf_op jit(solution)/shard_map/jit(cholesky)/cholesky | solution.py:32
  106.2 7.9 while.4
  106.8 1.3 bitcast_dynamic-update-slice_fusion.4
  108.8 1.3 bitcast_dynamic-update-slice_fusion.4
  110.8 1.3 bitcast_dynamic-update-slice_fusion.4
  112.7 1.3 bitcast_dynamic-update-slice_fusion.4
  114.0 39.3 %custom-call.32 = f32[4,128,128]{1,2,0:T(8,128)S(1)} custom-call(f32[4,128,128]{2,1,0:T(8,128)S(1)} %get-tuple-element.19), custom_call_target="InvertDiagBlocksLowerTriangular" | custom-call | tf_op jit(solution)/shard_map/jit(_cho_solve)/triangular_solve | solution.py:33
  162.4 56.1 %gather_fusion.1 = f32[8192,2,32]{2,1,0:T(2,128)} fusion(f32[1024,2,32]{2,1,0:T(2,128)S(1)} %copy.149, s32[8192]{0:T(1024)S(1)} %get-tuple-element.117), kind=kCustom, calls=%fused_computation.1.clone | custom fusion | bytes 4227072 | tf_op jit(solution)/shard_map/jit(_take)/gather | solution.py:43
  218.6 29.5 %broadcast_select_fusion.3 = f32[8192,2,32]{2,1,0:T(2,128)S(1)} fusion(f32[8192,2,32]{2,1,0:T(2,128)} %gather_fusion.1, pred[8192]{0:T(1024)(128)(4,1)S(1)} %get-tuple-element.115), kind=kLoop, calls=%fused_computation.13 | loop fusion | flops 524288 | bytes 4202496 | tf_op jit(solution)/shard_map/jit(_take)/select_n | solution.py:43
  248.1 7.7 fusion.142
  255.8 56.1 %gather_fusion = f32[8192,2,32]{2,1,0:T(2,128)} fusion(f32[1024,2,32]{2,1,0:T(2,128)S(1)} %copy.149, s32[8192]{0:T(1024)S(1)} %get-tuple-element.116), kind=kCustom, calls=%fused_computation.clone | custom fusion | bytes 4227072 | tf_op jit(solution)/shard_map/jit(_take)/gather | solution.py:43
  311.9 29.5 %broadcast_select_fusion.5 = f32[8192,2,32]{2,1,0:T(2,128)S(1)} fusion(f32[8192,2,32]{2,1,0:T(2,128)} %gather_fusion, pred[8192]{0:T(1024)(128)(4,1)S(1)} %compare_and_fusion.2), kind=kLoop, calls=%fused_computation.15 | loop fusion | flops 524288 | bytes 4202496 | tf_op jit(solution)/shard_map/jit(_take)/select_n | solution.py:43
  341.5 7.7 fusion.143
  349.1 56.1 %gather_fusion.2 = f32[8192,2,32]{2,1,0:T(2,128)} fusion(f32[1024,2,32]{2,1,0:T(2,128)S(1)} %copy.149, s32[8192]{0:T(1024)S(1)} %fusion.124), kind=kCustom, calls=%fused_computation.2.clone | custom fusion | bytes 4227072 | tf_op jit(solution)/shard_map/jit(_take)/gather | solution.py:43
  405.3 29.5 %broadcast_select_fusion.1 = f32[8192,2,32]{2,1,0:T(2,128)S(1)} fusion(f32[8192,2,32]{2,1,0:T(2,128)} %gather_fusion.2, pred[8192]{0:T(1024)(128)(4,1)S(1)} %get-tuple-element.114), kind=kLoop, calls=%fused_computation.11 | loop fusion | flops 524288 | bytes 4202496 | tf_op jit(solution)/shard_map/jit(_take)/select_n | solution.py:43
  434.8 7.7 fusion.141
  442.5 9.1 multiply_subtract_fusion.1
  451.6 7.0 fusion.3
  459.8 1.1 convert_element_type.37
  461.0 27.0 %all-gather.3.cloned.1.call-done = bf16[1024,512]{1,0:T(8,128)(2,1)} async-done(((bf16[128,512]{1,0:T(8,128)(2,1)}), bf16[1024,512]{1,0:T(8,128)(2,1)}) %all-gather.3.cloned.1.call-update) | async-done | bytes 1048592 | tf_op jit(solution)/shard_map/all_gather | solution.py:100
  490.5 11.7 %cholesky.358 = f32[128,128]{1,0:T(8,128)S(1)} custom-call(f32[128,128]{1,0:T(8,128)S(1)} %cholesky.439), custom_call_target="Cholesky" | custom-call | tf_op jit(solution)/shard_map/jit(cholesky)/cholesky | solution.py:32
  502.2 9.8 custom-call.33
  512.1 1.2 constant_dynamic-update-slice_fusion.2
  513.4 1.3 convolution_subtract_fusion
  514.7 11.7 %cholesky.377 = f32[128,128]{1,0:T(8,128)S(1)} custom-call(f32[128,128]{1,0:T(8,128)S(1)} %cholesky.443), custom_call_target="Cholesky" | custom-call | tf_op jit(solution)/shard_map/jit(cholesky)/cholesky | solution.py:32
  526.4 10.0 %custom-call.34 = f32[1,128,128]{1,2,0:T(8,128)S(1)} custom-call(f32[1,128,128]{2,1,0:T(8,128)S(1)} %get-tuple-element.102), custom_call_target="InvertDiagBlocksLowerTriangular" | custom-call | tf_op jit(solution)/shard_map/jit(cholesky)/cholesky | solution.py:32
  536.7 1.3 convolution_subtract_fusion.2
  538.0 11.7 %cholesky.398 = f32[128,128]{1,0:T(8,128)S(1)} custom-call(f32[128,128]{1,0:T(8,128)S(1)} %cholesky.448), custom_call_target="Cholesky" | custom-call | tf_op jit(solution)/shard_map/jit(cholesky)/cholesky | solution.py:32
  549.7 9.8 custom-call.35
  559.7 1.2 convolution_subtract_fusion.14
  561.0 11.7 %cholesky.415 = f32[128,128]{1,0:T(8,128)S(1)} custom-call(f32[128,128]{1,0:T(8,128)S(1)} %convolution_subtract_fusion.14), custom_call_target="Cholesky" | custom-call | tf_op jit(solution)/shard_map/jit(cholesky)/cholesky | solution.py:32
  577.6 23.8 %all-gather.5.cloned.1.call-done = bf16[16384,512]{1,0:T(8,128)(2,1)} async-done(((bf16[1024,512]{1,0:T(8,128)(2,1)}), bf16[16384,512]{1,0:T(8,128)(2,1)}) %all-gather.5.cloned.1.call-update) | async-done | bytes 16777232 | tf_op jit(solution)/shard_map/all_gather | solution.py:101
  601.4 5.2 fusion.8
  606.5 1.8 dynamic-slice_negate_fusion
  608.4 5.9 add_bitcast_fusion
  614.3 8.0 while.5
  614.9 1.4 bitcast_dynamic-update-slice_fusion.5
  616.9 1.4 bitcast_dynamic-update-slice_fusion.5
  618.9 1.4 bitcast_dynamic-update-slice_fusion.5
  620.9 1.4 bitcast_dynamic-update-slice_fusion.5
  622.3 39.3 %custom-call.36 = f32[4,128,128]{1,2,0:T(8,128)S(1)} custom-call(f32[4,128,128]{2,1,0:T(8,128)S(1)} %get-tuple-element.20), custom_call_target="InvertDiagBlocksLowerTriangular" | custom-call | tf_op jit(solution)/shard_map/jit(_cho_solve)/triangular_solve | solution.py:33
  662.1 16.2 %all-reduce.9.cloned.1.call-done = f32[1024,512]{0,1:T(8,128)} async-done(((f32[1024,512]{0,1:T(8,128)}), f32[1024,512]{0,1:T(8,128)}) %all-reduce.9.cloned.1.call-update) | async-done | bytes 2097168 | tf_op jit(solution)/shard_map/psum | solution.py:92
  685.0 56.1 %gather_fusion.4 = f32[8192,2,32]{2,1,0:T(2,128)} fusion(f32[1024,2,32]{2,1,0:T(2,128)S(1)} %copy.163, s32[8192]{0:T(1024)S(1)} %copy-done.19), kind=kCustom, calls=%fused_computation.4.clone | custom fusion | bytes 4227072 | tf_op jit(solution)/shard_map/jit(_take)/gather | solution.py:43
  741.2 56.1 %gather_fusion.3 = f32[8192,2,32]{2,1,0:T(2,128)} fusion(f32[1024,2,32]{2,1,0:T(2,128)S(1)} %copy.163, s32[8192]{0:T(1024)S(1)} %copy-done.17), kind=kCustom, calls=%fused_computation.3.clone | custom fusion | bytes 4227072 | tf_op jit(solution)/shard_map/jit(_take)/gather | solution.py:43
  797.3 56.1 %gather_fusion.5 = f32[8192,2,32]{2,1,0:T(2,128)} fusion(f32[1024,2,32]{2,1,0:T(2,128)S(1)} %copy.163, s32[8192]{0:T(1024)S(1)} %copy-done.15), kind=kCustom, calls=%fused_computation.5.clone | custom fusion | bytes 4227072 | tf_op jit(solution)/shard_map/jit(_take)/gather | solution.py:43
  853.4 29.5 %broadcast_select_fusion.2 = f32[8192,2,32]{2,1,0:T(2,128)S(1)} fusion(f32[8192,2,32]{2,1,0:T(2,128)} %gather_fusion.4, pred[8192]{0:T(1024)(128)(4,1)S(1)} %copy-done.26), kind=kLoop, calls=%fused_computation.12 | loop fusion | flops 524288 | bytes 4202496 | tf_op jit(solution)/shard_map/jit(_take)/select_n | solution.py:43
  883.0 7.5 fusion.139
  890.4 28.5 %broadcast_select_fusion.4 = f32[8192,2,32]{2,1,0:T(2,128)S(1)} fusion(f32[8192,2,32]{2,1,0:T(2,128)S(1)} %copy-done, pred[8192]{0:T(1024)(128)(4,1)S(1)} %copy-done.24), kind=kLoop, calls=%fused_computation.14 | loop fusion | flops 524288 | bytes 4202496 | tf_op jit(solution)/shard_map/jit(_take)/select_n | solution.py:43
  919.0 7.7 fusion.140
  926.7 28.8 %broadcast_select_fusion = f32[8192,2,32]{2,1,0:T(2,128)S(1)} fusion(f32[8192,2,32]{2,1,0:T(2,128)S(1)} %bitcast.259, pred[8192]{0:T(1024)(128)(4,1)S(1)} %get-tuple-element.114), kind=kLoop, calls=%fused_computation.10 | loop fusion | flops 524288 | bytes 4202496 | tf_op jit(solution)/shard_map/jit(_take)/select_n | solution.py:43
  955.5 7.7 fusion.138
  963.2 9.0 multiply_subtract_fusion
  972.2 7.0 fusion.1
  980.9 1.0 copy.175
  (204 shorter events, 37.0 us)
Async XLA Ops:
  7.2 2.6 copy-start.5
  7.2 146.4 %all-reduce.5.cloned.1.call-start = ((), (), s32[]{:S(2)}) async-start(), calls=%async_computation | async-start | bytes 2097152 | tf_op jit(solution)/shard_map/psum | solution.py:13
  9.7 145.0 %all-reduce.7.cloned.1.call-start = ((), (), s32[]{:S(2)}) async-start(), calls=%async_computation.1 | async-start | bytes 4194304 | tf_op jit(solution)/shard_map/psum | solution.py:92
  9.8 4.9 slice-start.2
  9.9 4.7 slice-start.3
  14.7 4.0 copy-start.6
  18.4 469.6 %all-gather.3.cloned.1.call-start = ((), (), s32[]{:S(2)}) async-start(), calls=%async_computation.2 | async-start | bytes 1179648 | tf_op jit(solution)/shard_map/all_gather | solution.py:100
  19.7 0.7 copy-start.3
  19.9 0.7 copy-start.4
  22.4 91.6 %copy-start.22 = (s32[3,8,1024]{2,1,0:T(8,128)S(1)}, s32[3,8,1024]{2,1,0:T(8,128)}, u32[]{:S(2)}) copy-start(s32[3,8,1024]{2,1,0:T(8,128)} %param.14) | copy-start | bytes 294916
  153.4 158.5 %copy-start.23 = (pred[8192]{0:T(1024)(128)(4,1)}, pred[8192]{0:T(1024)(128)(4,1)S(1)}, u32[]{:S(2)}) copy-start(pred[8192]{0:T(1024)(128)(4,1)S(1)} %compare_and_fusion.2) | copy-start | bytes 24580
  153.4 195.7 %copy-start.14 = (s32[8192]{0:T(1024)}, s32[8192]{0:T(1024)S(1)}, u32[]{:S(2)}) copy-start(s32[8192]{0:T(1024)S(1)} %fusion.124) | copy-start | bytes 98308
  153.5 65.1 %copy-start.25 = (pred[8192]{0:T(1024)(128)(4,1)}, pred[8192]{0:T(1024)(128)(4,1)S(1)}, u32[]{:S(2)}) copy-start(pred[8192]{0:T(1024)(128)(4,1)S(1)} %get-tuple-element.115) | copy-start | bytes 24580
  153.5 8.9 copy-start.18
  153.5 102.3 %copy-start.16 = (s32[8192]{0:T(1024)}, s32[8192]{0:T(1024)S(1)}, u32[]{:S(2)}) copy-start(s32[8192]{0:T(1024)S(1)} %get-tuple-element.116) | copy-start | bytes 98308
  159.3 1.5 copy-start.8
  160.1 0.8 copy-start.12
  434.8 7.7 copy-start.1
  442.5 9.1 copy-start.20
  458.6 29.9 %copy-start.11 = (f32[1,1,256,256]{3,2,1,0:T(8,128)S(1)}, f32[1,1,256,256]{3,2,1,0:T(8,128)}, u32[]{:S(2)}) copy-start(f32[1,1,256,256]{3,2,1,0:T(8,128)} %get-tuple-element.78) | copy-start | bytes 786436
  458.6 30.0 %copy-start.10 = (f32[1,1,256,256]{3,2,1,0:T(8,128)S(1)}, f32[1,1,256,256]{3,2,1,0:T(8,128)}, u32[]{:S(2)}) copy-start(f32[1,1,256,256]{3,2,1,0:T(8,128)} %get-tuple-element.76) | copy-start | bytes 786436
  461.0 140.4 %all-gather.5.cloned.1.call-start = ((), (), s32[]{:S(2)}) async-start(), calls=%async_computation.3 | async-start | bytes 17825792 | tf_op jit(solution)/shard_map/all_gather | solution.py:101
  488.0 190.3 %all-reduce.9.cloned.1.call-start = ((), (), s32[]{:S(2)}) async-start(), calls=%async_computation.4 | async-start | bytes 4194304 | tf_op jit(solution)/shard_map/psum | solution.py:92
  489.4 1.0 copy-start.2
  608.3 70.0 %copy-start.9 = (f32[128,128]{1,0:T(8,128)S(1)}, f32[128,128]{1,0:T(8,128)}, u32[]{:S(2)}) copy-start(f32[128,128]{1,0:T(8,128)} %copy-done.8) | copy-start | bytes 196612
  608.3 70.0 %copy-start.13 = (f32[128,128]{1,0:T(8,128)S(1)}, f32[128,128]{1,0:T(8,128)}, u32[]{:S(2)}) copy-start(f32[128,128]{1,0:T(8,128)} %copy-done.12) | copy-start | bytes 196612
  681.8 3.2 copy-start.19
  685.0 56.2 %copy-start.17 = (s32[8192]{0:T(1024)S(1)}, s32[8192]{0:T(1024)}, u32[]{:S(2)}) copy-start(s32[8192]{0:T(1024)} %copy-done.16) | copy-start | bytes 98308
  741.2 56.1 %copy-start.15 = (s32[8192]{0:T(1024)S(1)}, s32[8192]{0:T(1024)}, u32[]{:S(2)}) copy-start(s32[8192]{0:T(1024)} %copy-done.14) | copy-start | bytes 98308
  797.3 56.1 %copy-start.26 = (pred[8192]{0:T(1024)(128)(4,1)S(1)}, pred[8192]{0:T(1024)(128)(4,1)}, u32[]{:S(2)}) copy-start(pred[8192]{0:T(1024)(128)(4,1)} %copy-done.25) | copy-start | bytes 24580
  882.9 7.5 copy-start
  883.0 7.5 copy-start.24
  883.0 43.7 %slice-start = ((s8[8388608]{0:T(1024)(128)(4,1)}), s8[4194304]{0:T(1024)(128)(4,1)S(1)}, s32[]{:S(2)}) async-start(s8[8388608]{0:T(1024)(128)(4,1)} %bitcast.258), calls=%async_computation.5 | async-start | bytes 8388608
  890.4 36.3 %slice-start.1 = ((s8[8388608]{0:T(1024)(128)(4,1)}), s8[4194304]{0:T(1024)(128)(4,1)S(1)}, s32[]{:S(2)}) async-start(s8[8388608]{0:T(1024)(128)(4,1)} %bitcast.258), calls=%async_computation.6 | async-start | bytes 8388608
  963.2 9.0 copy-start.21
  979.2 1.7 copy-start.7
Sparse Core Ops, SparseCore 0:
  10.4 63.9 all-reduce.4
  76.8 65.5 all-reduce.6
  461.1 26.8 all-gather.2
  490.0 111.3 all-gather.4
  614.4 63.8 all-reduce.8
where the time goes:
time: 995 us; the launch traced here: 990 us
  other arithmetic  455 us (46%)
  local copies, waits for them, and re-layouts  411 us (41%)
  waiting for transfers between devices  67.2 us (7%)
  matrix products  35 us (4%)
  between operations  20.5 us (2%)
    gather x6, local copies, waits for them, and re-layouts, select_pairs(): taken = jnp.take(field, pair_index[which].reshape(-1), axis=0)  337 us
    select_n x6, other arithmetic, select_pairs(): taken = jnp.take(field, pair_index[which].reshape(-1), axis=0)  175 us
    another operation x28, other arithmetic, block_solve(): jnp.linalg.cholesky(jnp.concatenate([upper_half, lower_half], axis=0))  158 us
    another operation x5, other arithmetic, block_solve(): return jax.scipy.linalg.cho_solve((factor, True), rhs_rows.T).T  78.9 us
    all_gather x1, waiting for transfers between devices, per_device(): column_rows = lax.all_gather(sigma_new, 'hist', axis=0, tiled=True)  27 us
    all_gather x1, waiting for transfers between devices, per_device(): every_row = lax.all_gather(column_rows, 'tsec', axis=0, tiled=True)  23.8 us
  transfers between devices with their start and end apart: 5, of which 3 were waited for; matrix products, arithmetic and copies ran while one was open for 28% of the time, Pallas kernels for 0%

commit v1 on v0

v1 whole, which is shorter than its diff:
```python
import functools

import jax
import jax.numpy as jnp
from jax import lax
from jax.experimental import pallas as pl
from jax.experimental.pallas import tpu as pltpu
from jax.sharding import PartitionSpec as P

N = 32
B = 8
NBLK = 2
Q = 8
HALF = B * N
WIDE = 2 * HALF
LANES = 128
PAIRS = N * N
TILES = PAIRS // LANES
MESH = pl.DeviceIdType.MESH
f32, bf16, i32 = jnp.float32, jnp.bfloat16, jnp.int32
HIGHEST = lax.Precision.HIGHEST
PEAK = 32000.0


def dot(left, right, precision=None):
    return jnp.dot(left, right, preferred_element_type=f32, precision=precision)


def inverse_kernel(op_ref, out_ref, a_ref, x_ref, r_ref):
    block = pl.program_id(0)
    rows = lax.broadcasted_iota(i32, (HALF, HALF), 0)
    cols = lax.broadcasted_iota(i32, (HALF, HALF), 1)
    eye = jnp.where(rows == cols, 1.0, 0.0).astype(f32)
    real, imag = op_ref[block, 0], op_ref[block, 1]
    a_ref[0], a_ref[1] = real, imag
    inv_row = 1.0 / jnp.sum(real * eye, axis=0, keepdims=True)
    r_ref[0] = eye - real * inv_row
    r_ref[1] = -imag * inv_row
    x_ref[0] = eye * inv_row
    x_ref[1] = jnp.zeros((HALF, HALF), f32)

    def worst():
        return jnp.max(jnp.maximum(jnp.abs(r_ref[0]), jnp.abs(r_ref[1])))

    def unfinished(carry):
        step, size = carry
        return jnp.logical_and(step < 40, size > 1e-6)

    def improve(carry):
        step, _ = carry
        xr, xi, rr, ri = x_ref[0], x_ref[1], r_ref[0], r_ref[1]
        x_ref[0] = xr + (dot(xr, rr, HIGHEST) - dot(xi, ri, HIGHEST))
        x_ref[1] = xi + (dot(xr, ri, HIGHEST) + dot(xi, rr, HIGHEST))
        xr, xi, ar, ai = x_ref[0], x_ref[1], a_ref[0], a_ref[1]
        r_ref[0] = eye - (dot(ar, xr, HIGHEST) - dot(ai, xi, HIGHEST))
        r_ref[1] = -(dot(ar, xi, HIGHEST) + dot(ai, xr, HIGHEST))
        return step + 1, worst()

    lax.while_loop(unfinished, improve, (jnp.int32(0), worst()))
    xr, xi = x_ref[0], x_ref[1]
    out_ref[0, :HALF, :HALF] = xr
    out_ref[0, :HALF, HALF:] = -xi
    out_ref[0, HALF:, :HALF] = xi
    out_ref[0, HALF:, HALF:] = xr


def invert(step_operator):
    return pl.pallas_call(
        inverse_kernel,
        grid=(NBLK,),
        out_shape=jax.ShapeDtypeStruct((NBLK, WIDE, WIDE), f32),
        in_specs=[pl.BlockSpec(memory_space=pltpu.VMEM)],
        out_specs=pl.BlockSpec((1, WIDE, WIDE), lambda k: (k, 0, 0)),
        scratch_shapes=[pltpu.VMEM((2, HALF, HALF), f32)] * 3,
        compiler_params=pltpu.CompilerParams(vmem_limit_bytes=32 << 20),
    )(step_operator)


def window_kernel(
    green_hbm, panel_ref, inv_ref, pair_ref, weight_ref,
    rows_ref, sigma_ref,
    green, panel_next, held, field, packed, spread, sig, sigma_out,
    sib_send, sib_recv, sums, hop_recv, end_recv,
    load_sem, sib_ss, sib_rs, hop_ss, hop_rs, end_ss, end_rs, gat_ss, gat_rs, gat_ls,
):
    hist, tsec = lax.axis_index("hist"), lax.axis_index("tsec")
    chip, core = hist // 2, hist % 2
    right = ((chip + 1) % 4) * 2 + core
    left = ((chip + 3) % 4) * 2 + core
    sibling = chip * 2 + 1 - core
    target = tsec // 2

    def loads(d):
        lanes = pl.ds(pl.multiple_of(d * LANES, LANES), LANES)
        return [
            pltpu.make_async_copy(
                green_hbm.at[part, :, lanes],
                green.at[d, :, pl.ds(part * LANES, LANES)],
                load_sem.at[d, part],
            )
            for part in range(2)
        ]

    for o in (2, 1, 3, 0):
        for d in (((chip + o) % 4) * 2 + 1 - core, ((chip + o) % 4) * 2 + core):
            for copy in loads(d):
                copy.start()

    barrier = pltpu.get_barrier_semaphore()
    for h in (right, left, sibling):
        pl.semaphore_signal(barrier, inc=1, device_id={"hist": h, "tsec": tsec}, device_id_type=MESH)
    for h in range(8):
        for odd in range(2):
            source = 2 * hist + odd
            @pl.when(jnp.logical_or(source != tsec, hist != h))
            def _():
                pl.semaphore_signal(barrier, inc=1, device_id={"hist": h, "tsec": source}, device_id_type=MESH)
    pl.semaphore_wait(barrier, jnp.where(target == hist, 18, 19))

    is_last = jnp.where(hist == 7, 1.0, 0.0).astype(f32)

    def remote(src, dst, ss, rs, h):
        return pltpu.make_async_remote_copy(
            src_ref=src, dst_ref=dst, send_sem=ss, recv_sem=rs,
            device_id={"hist": h, "tsec": tsec}, device_id_type=MESH,
        )

    def memory(k, panel):
        top, low = pl.ds(0, HALF), pl.ds(HALF, HALF)

        def chunk(d):
            out = dot(panel[...], green[d])
            re = out[:HALF, :LANES] - out[HALF:, LANES:]
            im = out[HALF:, :LANES] + out[:HALF, LANES:]
            if k == 0:
                tail = green[d, green.shape[1] - HALF :, :].astype(f32) * is_last
                re, im = re + tail[:, :LANES], im + tail[:, LANES:]
            return re, im

        hop_a = remote(sums.at[k, 0, top], hop_recv.at[k, top], hop_ss.at[k, 0], hop_rs.at[k, 0], right)
        hop_b = remote(sums.at[k, 0, low], hop_recv.at[k, low], hop_ss.at[k, 1], hop_rs.at[k, 1], left)
        end_a = remote(sums.at[k, 1], end_recv.at[k, 0], end_ss.at[k, 0], end_rs.at[k, 0], right)
        end_b = remote(sums.at[k, 2], end_recv.at[k, 1], end_ss.at[k, 1], end_rs.at[k, 1], left)

        def step(i, carry):
            o = jnp.where(i == 0, 2, jnp.where(i == 1, 1, jnp.where(i == 2, 3, 0)))
            base = ((chip + o) % 4) * 2
            far, near = base + 1 - core, base + core
            if k == 0:
                for copy in loads(far):
                    copy.wait()
            re, im = chunk(far)
            sib_send[k, i, :HALF] = re
            sib_send[k, i, HALF:] = im
            swap = remote(sib_send.at[k, i], sib_recv.at[k, i], sib_ss.at[k, i], sib_rs.at[k, i], sibling)
            swap.start()
            if k == 0:
                for copy in loads(near):
                    copy.wait()
            re, im = chunk(near)
            swap.wait()
            sums[k, i, :HALF] = re + sib_recv[k, i, :HALF]
            sums[k, i, HALF:] = im + sib_recv[k, i, HALF:]

            @pl.when(i == 0)
            def _():
                hop_a.start()
                hop_b.start()

            @pl.when(i == 1)
            def _():
                hop_a.wait_recv()
                sums[k, 1, :HALF] = sums[k, 1, :HALF] + hop_recv[k, :HALF]
                end_a.start()

            @pl.when(i == 2)
            def _():
                hop_b.wait_recv()
                sums[k, 2, HALF:] = sums[k, 2, HALF:] + hop_recv[k, HALF:]
                end_b.start()

            return carry

        lax.fori_loop(0, 4, step, 0)
        end_a.wait_recv()
        end_b.wait_recv()
        for copy in (hop_a, hop_b, end_a, end_b):
            copy.wait_send()
        return sums[k, 3] + end_recv[k, 0] + end_recv[k, 1]

    lane_group = lax.broadcasted_iota(i32, (LANES, LANES), 1) // N

    def regroup(pick, store):
        for s in range(4):
            value = None
            for a in range(4):
                moved = pick(a)
                if a != s:
                    moved = pltpu.roll(moved, (N * (a - s)) % LANES, 1)
                value = moved if value is None else jnp.where(lane_group == a, moved, value)
            store(s, value)

    def self_energy(k):
        peak = jnp.maximum(jnp.max(jnp.abs(held[...])), 1e-30)
        scale, unit = PEAK / peak, peak / PEAK

        def store_field(s, value):
            whole = jnp.round(value * scale).astype(i32)
            both = lax.shift_left(whole[:64], 16) | (whole[64:] & 0xFFFF)
            field[s] = both
        regroup(lambda a: held[pl.ds(a, LANES, stride=4), :], store_field)
        for j in range(TILES):
            for s in range(4):
                packed[j, s] = field[s, pl.ds(j, 8, stride=TILES), :]

        def tile(j, carry):
            def term(q, acc):
                values = []
                for f in range(3):
                    pair = pair_ref[j, f * Q + q]
                    low, high = pair & (LANES - 1), lax.shift_right_logical(pair, 7)
                    masks = [high == n for n in range(1, TILES)]
                    parts = []
                    for s in range(4):
                        found = jnp.take_along_axis(packed[0, s], low, axis=1)
                        for n in range(1, TILES):
                            found = jnp.where(masks[n - 1], jnp.take_along_axis(packed[n, s], low, axis=1), found)
                        parts.append((
                            lax.shift_right_arithmetic(found, 16).astype(f32),
                            lax.shift_right_arithmetic(lax.shift_left(found, 16), 16).astype(f32),
                        ))
                    values.append(parts)
                weight = weight_ref[j, q]
                result = []
                for s in range(4):
                    (ar, ai), (br, bi), (cr, ci) = values[0][s], values[1][s], values[2][s]
                    pr, pi = ar * br - ai * bi, ar * bi + ai * br
                    result.append(acc[2 * s] + weight * (pr * cr + pi * ci))
                    result.append(acc[2 * s + 1] + weight * (pi * cr - pr * ci))
                return tuple(result)

            acc = lax.fori_loop(0, Q, term, tuple(jnp.zeros((8, LANES), f32) for _ in range(8)), unroll=2)
            for s in range(4):
                for part in range(2):
                    spread[s, j, part * 8 : part * 8 + 8, :] = acc[2 * s + part] * (unit * unit * unit)
            return carry

        lax.fori_loop(0, TILES, tile, 0)

        def store_sigma(a, value):
            sig[pl.ds(a, LANES, stride=4), :] = value
        for s in range(4):
            for j in range(TILES):
                for part in range(2):
                    held_rows = pl.ds(part * 64 + j, 8, stride=TILES)
                    sib_send[k, s, held_rows, :] = spread[s, j, part * 8 : part * 8 + 8, :]
        regroup(lambda s: sib_send[k, s, :LANES, :], store_sigma)

    def gather_copy(o):
        slot = (tsec % 2) * 8 + hist
        there = panel_next.at[:, pl.ds(pl.multiple_of(slot * LANES, LANES), LANES)]
        return pltpu.make_async_remote_copy(
            src_ref=sigma_out, dst_ref=there, send_sem=gat_ss.at[o], recv_sem=gat_rs.at[slot],
            device_id={"hist": target, "tsec": (tsec + o) % 16}, device_id_type=MESH,
        )

    def own_copy():
        slot = (tsec % 2) * 8 + hist
        there = panel_next.at[:, pl.ds(pl.multiple_of(slot * LANES, LANES), LANES)]
        return pltpu.make_async_copy(sigma_out, there, gat_ls)

    for k in range(NBLK):
        total = memory(k, panel_ref if k == 0 else panel_next)
        rhs = total if k == 0 else total + held[...]
        solved = dot(inv_ref[k], rhs, HIGHEST)
        held[...] = solved
        rows_ref[k] = solved.T
        self_energy(k)
        if k + 1 < NBLK:
            sigma_out[...] = sig[...].astype(bf16)
            for o in range(1, 16):
                gather_copy(o).start()

            @pl.when(target != hist)
            def _():
                gather_copy(0).start()

            @pl.when(target == hist)
            def _():
                own_copy().start()
        sigma_ref[k] = sig[...].T.astype(bf16)
        if k + 1 < NBLK:
            own_slot = (tsec % 2) * 8 + hist
            for slot in range(16):
                there = panel_next.at[:, pl.ds(slot * LANES, LANES)]
                arrived = pltpu.make_async_remote_copy(
                    src_ref=sigma_out, dst_ref=there, send_sem=gat_ss.at[0], recv_sem=gat_rs.at[slot],
                    device_id={"hist": sibling, "tsec": tsec}, device_id_type=MESH,
                )

                @pl.when(jnp.logical_or(target != hist, own_slot != slot))
                def _():
                    arrived.wait_recv()

            @pl.when(target == hist)
            def _():
                own_copy().wait()
            for o in range(1, 16):
                gather_copy(o).wait_send()

            @pl.when(target != hist)
            def _():
                gather_copy(0).wait_send()


def per_device(hist_green, sigma_panel, step_operator, coupling, pair_index):
    inverse = invert(step_operator)
    pairs = pair_index.reshape(3 * Q, TILES, LANES).transpose(1, 0, 2)
    pairs = jnp.broadcast_to(pairs[:, :, None], (TILES, 3 * Q, 8, LANES))
    weights = coupling.reshape(Q, TILES, LANES).transpose(1, 0, 2)
    weights = jnp.broadcast_to(weights[:, :, None], (TILES, Q, 8, LANES))
    panel = sigma_panel.T
    depth = panel.shape[1]
    vmem = pl.BlockSpec(memory_space=pltpu.VMEM)
    dma = pltpu.SemaphoreType.DMA
    rows, sigma = pl.pallas_call(
        window_kernel,
        out_shape=(
            jax.ShapeDtypeStruct((NBLK, LANES, WIDE), f32),
            jax.ShapeDtypeStruct((NBLK, LANES, WIDE), bf16),
        ),
        in_specs=[pl.BlockSpec(memory_space=pl.ANY)] + [vmem] * 4,
        out_specs=(vmem, vmem),
        scratch_shapes=[
            pltpu.VMEM((8, depth, 2 * LANES), bf16),
            pltpu.VMEM((WIDE, depth), bf16),
            pltpu.VMEM((WIDE, LANES), f32),
            pltpu.VMEM((4, 64, LANES), i32),
            pltpu.VMEM((TILES, 4, 8, LANES), i32),
            pltpu.VMEM((4, TILES, 16, LANES), f32),
            pltpu.VMEM((WIDE, LANES), f32),
            pltpu.VMEM((WIDE, LANES), bf16),
            pltpu.VMEM((NBLK, 4, WIDE, LANES), f32),
            pltpu.VMEM((NBLK, 4, WIDE, LANES), f32),
            pltpu.VMEM((NBLK, 4, WIDE, LANES), f32),
            pltpu.VMEM((NBLK, WIDE, LANES), f32),
            pltpu.VMEM((NBLK, 2, WIDE, LANES), f32),
            dma((8, 2)),
            dma((NBLK, 4)), dma((NBLK, 4)),
            dma((NBLK, 2)), dma((NBLK, 2)),
            dma((NBLK, 2)), dma((NBLK, 2)),
            dma((16,)), dma((16,)), dma(()),
        ],
        compiler_params=pltpu.CompilerParams(
            collective_id=0, has_side_effects=True, vmem_limit_bytes=56 << 20
        ),
    )(hist_green, panel, inverse, pairs, weights)
    return rows[:, None], sigma[:, None]


def solution(mesh):
    return jax.shard_map(
        per_device,
        mesh=mesh,
        in_specs=(P(None, "hist", "tsec"), P("hist", None), P(), P(), P()),
        out_specs=(P(None, "tsec", "hist", None), P(None, "tsec", "hist", None)),
        check_vma=False,
    )
```

time: 995 us -> 217 us (0.22)
  the two profiles are of different devices: /device:TPU:1 before, /device:TPU:34 now
where the time goes in v1:
time: 217 us
  Pallas kernels  204 us (94%)
  local copies, waits for them, and re-layouts  12.2 us (6%)
    pallas_call x1, Pallas kernels, per_device(): pl.pallas_call(window_kernel, out_shape=(jax.ShapeDtypeStruct((NBLK, LANE...  195 us
    unnamed x8, local copies, waits for them, and re-layouts  9.8 us
    pallas_call x1, Pallas kernels, invert(): pl.pallas_call(inverse_kernel, grid=(NBLK,), out_shape=jax.ShapeDtypeStru...  9.53 us

profile of v1, /device:TPU:34, one launch (start us, length us, event | category | flops | bytes accessed | tf_op | source)
XLA Modules:
  0.0 217.0 jit_solution(13309948458096869461)
XLA Ops:
  0.6 0.9 copy.11
  1.6 1.5 broadcast_in_dim.9.weight_ref
  3.1 0.9 broadcast_in_dim.8.pair_ref
  4.0 0.0 copy-start.1
  4.0 4.0 %copy.7 = bf16[2048,512]{0,1:T(8,128)(2,1)} copy(bf16[2048,512]{1,0:T(8,128)(2,1)} %param.6) | data formatting | bytes 4194304 | tf_op args[1]
  8.0 0.0 copy-done.1
  8.0 9.5 %shard_map.68.inv_ref = f32[2,512,512]{2,1,0:T(8,128)S(1)} custom-call(f32[2,2,256,256]{3,2,1,0:T(8,128)S(1)} %copy-done.1), custom_call_target="tpu_custom_call" | custom-call | tf_op jit(solution)/shard_map/pallas_call | solution.py:68
  17.6 0.0 copy-start
  17.6 1.3 copy-done
  18.9 194.6 %shard_map.69 = (f32[2,128,512]{2,1,0:T(8,128)}, bf16[2,128,512]{2,1,0:T(8,128)(2,1)}) custom-call(bf16[2,2048,1024]{2,1,0:T(8,128)(2,1)} %green_hbm.1, bf16[512,2048]{1,0:T(8,128)(2,1)} %bitcast.16, f32[2,512,512]{2,1,0:T(8,128)} %copy-done, s32[8,24,8,128]{3,2,1,0:T(8,128)} %broadcast_in_dim.8.pair_ref, f32[8,8,8,128]{3,2,1,0:T(8,128)} %broadcast_in_dim.9.weight_ref), custom_call_target="tpu_custom_call" | custom-call | tf_op jit(solution)/shard_map/pallas_call | solution.py:326
  213.5 1.9 copy.16
  215.3 1.7 copy.17
  (1 shorter events, 0.0 us)
Async XLA Ops:
  4.0 4.0 %copy-start.1 = (f32[2,2,256,256]{3,2,1,0:T(8,128)S(1)}, f32[2,2,256,256]{3,2,1,0:T(8,128)}, u32[]{:S(2)}) copy-start(f32[2,2,256,256]{3,2,1,0:T(8,128)} %op_ref.1) | copy-start | bytes 3145732
  17.6 1.3 copy-start

commit v2 on v1

v2 whole, which is shorter than its diff:
```python
import functools

import jax
import jax.numpy as jnp
from jax import lax
from jax.experimental import pallas as pl
from jax.experimental.pallas import tpu as pltpu
from jax.sharding import PartitionSpec as P

N = 32
B = 8
NBLK = 2
Q = 8
HALF = B * N
WIDE = 2 * HALF
LANES = 128
PAIRS = N * N
TILES = PAIRS // LANES
MESH = pl.DeviceIdType.MESH
f32, bf16, i32 = jnp.float32, jnp.bfloat16, jnp.int32
HIGHEST = lax.Precision.HIGHEST
PEAK = 32000.0


def dot(left, right, precision=None):
    return jnp.dot(left, right, preferred_element_type=f32, precision=precision)


def inverse_kernel(op_ref, out_ref, x_ref, r_ref):
    block = pl.program_id(0)
    rows = lax.broadcasted_iota(i32, (HALF, HALF), 0)
    cols = lax.broadcasted_iota(i32, (HALF, HALF), 1)
    eye = jnp.where(rows == cols, 1.0, 0.0).astype(f32)
    ar, ai = op_ref[block, 0], op_ref[block, 1]
    inv_row = 1.0 / jnp.sum(ar * eye, axis=0, keepdims=True)
    inv_col = 1.0 / jnp.sum(ar * eye, axis=1, keepdims=True)
    x_ref[0] = inv_col * (eye + (eye - ar * inv_row))
    x_ref[1] = inv_col * (-ai * inv_row)

    def residual():
        ar, ai, xr, xi = op_ref[block, 0], op_ref[block, 1], x_ref[0], x_ref[1]
        r_ref[0] = eye - (dot(ar, xr, HIGHEST) - dot(ai, xi, HIGHEST))
        r_ref[1] = -(dot(ar, xi, HIGHEST) + dot(ai, xr, HIGHEST))
        return jnp.max(jnp.sum(jnp.abs(r_ref[0]) + jnp.abs(r_ref[1]), axis=0, keepdims=True))

    def improve(precision):
        xr, xi, rr, ri = x_ref[0], x_ref[1], r_ref[0], r_ref[1]
        x_ref[0] = xr + (dot(xr, rr, precision) - dot(xi, ri, precision))
        x_ref[1] = xi + (dot(xr, ri, precision) + dot(xi, rr, precision))

    def unfinished(carry):
        step, norm = carry
        return jnp.logical_and(step < 40, norm > 3e-3)

    def again(carry):
        improve(HIGHEST)
        return carry[0] + 1, residual()

    lax.while_loop(unfinished, again, (jnp.int32(0), residual()))
    improve(None)
    xr, xi = x_ref[0], x_ref[1]
    out_ref[0, :HALF, :HALF] = xr
    out_ref[0, :HALF, HALF:] = -xi
    out_ref[0, HALF:, :HALF] = xi
    out_ref[0, HALF:, HALF:] = xr


def invert(step_operator):
    return pl.pallas_call(
        inverse_kernel,
        grid=(NBLK,),
        out_shape=jax.ShapeDtypeStruct((NBLK, WIDE, WIDE), f32),
        in_specs=[pl.BlockSpec(memory_space=pltpu.VMEM)],
        out_specs=pl.BlockSpec((1, WIDE, WIDE), lambda k: (k, 0, 0)),
        scratch_shapes=[pltpu.VMEM((2, HALF, HALF), f32)] * 2,
        compiler_params=pltpu.CompilerParams(vmem_limit_bytes=32 << 20),
    )(step_operator)


def window_kernel(
    green_hbm, panel_hbm, inv_hbm, pair_ref, weight_ref,
    rows_ref, sigma_ref,
    pair_wide, weight_wide,
    green, panel_raw, panel_now, panel_next, inv_ref, held, field, packed, spread, sig, sigma_out,
    sib_send, sib_recv, sums, msg_send, msg_recv, unit_send, unit_recv,
    load_sem, in_sem, sib_ss, sib_rs, msg_ss, msg_rs, unit_ss, unit_rs,
    st_ss, st_rs, st_ls, a1_ss, a1_rs, a2_ss, a2_rs, b1_ss, b1_rs, b2_ss, b2_rs,
):
    hist, tsec = lax.axis_index("hist"), lax.axis_index("tsec")
    chip, core = hist // 2, hist % 2
    z, y = tsec // 4, tsec % 4
    sibling = chip * 2 + 1 - core
    holder = core == y // 2
    depth = panel_now.shape[1]

    def at_chip(o, which):
        return ((chip + o) % 4) * 2 + which

    def loads(d):
        lanes = pl.ds(pl.multiple_of(d * LANES, LANES), LANES)
        return [
            pltpu.make_async_copy(
                green_hbm.at[part, :, lanes],
                green.at[d, :, pl.ds(part * LANES, LANES)],
                load_sem.at[d, part],
            )
            for part in range(2)
        ]

    panel_load = pltpu.make_async_copy(panel_hbm, panel_raw, in_sem.at[0])
    inv_load = pltpu.make_async_copy(inv_hbm, inv_ref, in_sem.at[1])
    panel_load.start()
    for o in (2, 1, 3, 0):
        for d in (at_chip(o, 1 - core), at_chip(o, core)):
            for copy in loads(d):
                copy.start()
    inv_load.start()

    barrier = pltpu.get_barrier_semaphore()

    def greet(h, t):
        pl.semaphore_signal(barrier, inc=1, device_id={"hist": h, "tsec": t}, device_id_type=MESH)

    greet(sibling, tsec)
    for o in range(1, 4):
        greet(at_chip(o, core), tsec)
        greet(hist, z * 4 + (y + o) % 4)
        greet(hist, ((z + o) % 4) * 4 + y)
    for h in range(8):
        @pl.when(jnp.logical_and(holder, jnp.logical_or(hist != h, z != chip)))
        def _():
            greet(h, chip * 4 + y)

    for j in range(TILES):
        lanes = slice(j * LANES, (j + 1) * LANES)
        for r in range(3 * Q):
            pair_wide[j, r] = jnp.broadcast_to(pair_ref[r : r + 1, lanes], (8, LANES))
        for r in range(Q):
            weight_wide[j, r] = jnp.broadcast_to(weight_ref[r : r + 1, lanes], (8, LANES))

    panel_load.wait()
    for r in range(depth // HALF):
        panel_now[:, r * HALF : (r + 1) * HALF] = panel_raw[r * HALF : (r + 1) * HALF, :].T
    own_part = hist == 2 * z + y // 2
    pl.semaphore_wait(barrier, jnp.where(own_part, 13, 14))

    is_last = jnp.where(hist == 7, 1.0, 0.0).astype(f32)

    def remote(src, dst, ss, rs, h, t):
        return pltpu.make_async_remote_copy(
            src_ref=src, dst_ref=dst, send_sem=ss, recv_sem=rs,
            device_id={"hist": h, "tsec": t}, device_id_type=MESH,
        )

    def memory(k, panel):
        def chunk(d):
            out = dot(panel[...], green[d])
            re = out[:HALF, :LANES] - out[HALF:, LANES:]
            im = out[HALF:, :LANES] + out[:HALF, LANES:]
            if k == 0:
                tail = green[d, green.shape[1] - HALF :, :].astype(f32) * is_last
                re, im = re + tail[:, :LANES], im + tail[:, LANES:]
            return re, im

        def swap(i):
            return remote(sib_send.at[k, i], sib_recv.at[k, i], sib_ss.at[k, i], sib_rs.at[k, i], sibling, tsec)

        def messages(o):
            there = at_chip(o, core)
            return (
                remote(msg_send.at[k, o - 1], msg_recv.at[k, o - 1], msg_ss.at[k, o - 1], msg_rs.at[k, o - 1], there, tsec),
                remote(unit_send.at[k, o - 1], unit_recv.at[k, o - 1], unit_ss.at[k, o - 1], unit_rs.at[k, o - 1], there, tsec),
            )

        def offset(i):
            return jnp.where(i == 0, 2, jnp.where(i == 1, 1, jnp.where(i == 2, 3, 0)))

        def step(i, carry):
            @pl.when(i < 4)
            def _():
                far = at_chip(offset(i), 1 - core)
                if k == 0:
                    for copy in loads(far):
                        copy.wait()
                re, im = chunk(far)
                sib_send[k, i, :HALF] = re
                sib_send[k, i, HALF:] = im
                swap(i).start()

            @pl.when(i > 0)
            def _():
                last = i - 1
                swap(last).wait()

                @pl.when(last < 3)
                def _():
                    o = offset(last)
                    re = sums[k, last, :HALF] + sib_recv[k, last, :HALF]
                    im = sums[k, last, HALF:] + sib_recv[k, last, HALF:]
                    peak = jnp.maximum(jnp.max(jnp.maximum(jnp.abs(re), jnp.abs(im))), 1e-30)
                    scale = PEAK / peak
                    high = jnp.round(re * scale).astype(i32)
                    low = jnp.round(im * scale).astype(i32)
                    msg_send[k, o - 1] = lax.shift_left(high, 16) | (low & 0xFFFF)
                    unit_send[k, o - 1] = jnp.full((8, LANES), 1.0, f32) * (peak / PEAK)
                    for copy in messages(o):
                        copy.start()

            @pl.when(i < 4)
            def _():
                near = at_chip(offset(i), core)
                if k == 0:
                    for copy in loads(near):
                        copy.wait()
                re, im = chunk(near)
                sums[k, i, :HALF] = re
                sums[k, i, HALF:] = im

            return carry

        lax.fori_loop(0, 5, step, 0)
        re = sums[k, 3, :HALF] + sib_recv[k, 3, :HALF]
        im = sums[k, 3, HALF:] + sib_recv[k, 3, HALF:]
        for o in (1, 3, 2):
            for copy in messages(o):
                copy.wait()
            both = msg_recv[k, o - 1]
            unit = unit_recv[k, o - 1, :1, :1]
            re = re + lax.shift_right_arithmetic(both, 16).astype(f32) * unit
            im = im + lax.shift_right_arithmetic(lax.shift_left(both, 16), 16).astype(f32) * unit
        return jnp.concatenate([re, im], axis=0)

    lane_group = lax.broadcasted_iota(i32, (LANES, LANES), 1) // N

    def regroup(pick, store):
        for s in range(4):
            value = None
            for a in range(4):
                moved = pick(a)
                if a != s:
                    moved = pltpu.roll(moved, (N * (a - s)) % LANES, 1)
                value = moved if value is None else jnp.where(lane_group == a, moved, value)
            store(s, value)

    def self_energy(k):
        peak = jnp.maximum(jnp.max(jnp.abs(held[...])), 1e-30)
        scale, unit = PEAK / peak, peak / PEAK

        def store_field(s, value):
            whole = jnp.round(value * scale).astype(i32)
            both = lax.shift_left(whole[:64], 16) | (whole[64:] & 0xFFFF)
            field[s] = both
        regroup(lambda a: held[pl.ds(a, LANES, stride=4), :], store_field)
        for j in range(TILES):
            for s in range(4):
                packed[j, s] = field[s, pl.ds(j, 8, stride=TILES), :]

        def tile(j, carry):
            def term(q, acc):
                values = []
                for f in range(3):
                    pair = pair_wide[j, f * Q + q]
                    low, high = pair & (LANES - 1), lax.shift_right_logical(pair, 7)
                    masks = [high == n for n in range(1, TILES)]
                    parts = []
                    for s in range(4):
                        found = jnp.take_along_axis(packed[0, s], low, axis=1)
                        for n in range(1, TILES):
                            found = jnp.where(masks[n - 1], jnp.take_along_axis(packed[n, s], low, axis=1), found)
                        parts.append((
                            lax.shift_right_arithmetic(found, 16).astype(f32),
                            lax.shift_right_arithmetic(lax.shift_left(found, 16), 16).astype(f32),
                        ))
                    values.append(parts)
                weight = weight_wide[j, q]
                result = []
                for s in range(4):
                    (ar, ai), (br, bi), (cr, ci) = values[0][s], values[1][s], values[2][s]
                    pr, pi = ar * br - ai * bi, ar * bi + ai * br
                    result.append(acc[2 * s] + weight * (pr * cr + pi * ci))
                    result.append(acc[2 * s + 1] + weight * (pi * cr - pr * ci))
                return tuple(result)

            acc = lax.fori_loop(0, Q, term, tuple(jnp.zeros((8, LANES), f32) for _ in range(8)), unroll=2)
            for s in range(4):
                for part in range(2):
                    spread[s, j, part * 8 : part * 8 + 8, :] = acc[2 * s + part] * (unit * unit * unit)
            return carry

        lax.fori_loop(0, TILES, tile, 0)

        def store_sigma(a, value):
            sig[pl.ds(a, LANES, stride=4), :] = value
        for s in range(4):
            for j in range(TILES):
                for part in range(2):
                    held_rows = pl.ds(part * 64 + j, 8, stride=TILES)
                    sib_send[k, s, held_rows, :] = spread[s, j, part * 8 : part * 8 + 8, :]
        regroup(lambda s: sib_send[k, s, :LANES, :], store_sigma)

    def first(j):
        slot = pl.ds(pl.multiple_of((y % 2) * 1024 + hist * LANES, LANES), LANES)
        rows = pl.ds(j * LANES, LANES)
        return remote(
            sigma_out.at[rows], panel_next.at[rows, slot], st_ss.at[j], st_rs.at[hist], 2 * z + y // 2, 4 * j + y
        )

    def first_here(j):
        slot = pl.ds(pl.multiple_of((y % 2) * 1024 + hist * LANES, LANES), LANES)
        rows = pl.ds(j * LANES, LANES)
        return pltpu.make_async_copy(sigma_out.at[rows], panel_next.at[rows, slot], st_ls)

    def piece(second, j, odd):
        rows = pl.ds(pl.multiple_of(j * LANES + second * 64, 64), 64)
        return panel_next.at[rows, pl.ds(pl.multiple_of(odd * 1024, 1024), 1024)]

    def pass_on(second, j, odd, ss, rs, t):
        return remote(piece(second, j, odd), piece(second, j, odd), ss, rs, hist, t)

    def along_y(n):
        return z * 4 + (y + n) % 4

    def along_z(n):
        return ((z + n) % 4) * 4 + y

    def a1(n):
        return pass_on(0, z, y % 2, a1_ss.at[n - 1], a1_rs.at[y % 2], along_y(n))

    def b1(n):
        return pass_on(1, z, y % 2, b1_ss.at[n - 1], b1_rs.at[z], along_z(n))

    def a2(odd, n):
        return pass_on(0, z, odd, a2_ss.at[odd, n - 1], a2_rs.at[z, odd], along_z(n))

    def b2(m, n):
        j = (z + m) % 4
        return pass_on(1, j, y % 2, b2_ss.at[m, n - 1], b2_rs.at[j, y % 2], along_y(n))

    def exchange():
        for j in range(4):
            here = jnp.logical_and(own_part, z == j)

            @pl.when(jnp.logical_not(here))
            def _():
                first(j).start()

            @pl.when(here)
            def _():
                first_here(j).start()

    def arrived(second, j, odd, rs):
        pass_on(second, j, odd, a1_ss.at[0], rs, along_y(1)).wait_recv()

    def relay():
        @pl.when(holder)
        def _():
            for h in range(8):
                slot = pl.ds(pl.multiple_of((y % 2) * 1024 + h * LANES, LANES), LANES)
                rows = pl.ds(pl.multiple_of(z * LANES, LANES), LANES)

                @pl.when(jnp.logical_or(hist != h, z != chip))
                def _():
                    remote(
                        sigma_out.at[pl.ds(0, LANES)], panel_next.at[rows, slot], st_ss.at[0], st_rs.at[h], sibling, tsec
                    ).wait_recv()

            for j in range(4):
                @pl.when(jnp.logical_and(own_part, z == j))
                def _():
                    first_here(j).wait()

            for n in (2, 1, 3):
                a1(n).start()
                b1(n).start()
            for n in (2, 1, 3):
                a2(y % 2, n).start()
                b2(0, n).start()

        for odd in range(2):
            @pl.when(2 * core + odd != y)
            def _():
                arrived(0, z, odd, a1_rs.at[odd])
                for n in (2, 1, 3):
                    a2(odd, n).start()

        @pl.when(holder)
        def _():
            for m in (1, 3, 2):
                j = (z + m) % 4
                arrived(1, j, y % 2, b1_rs.at[j])
                for n in (2, 1, 3):
                    b2(m, n).start()

    def settle():
        for odd in range(2):
            for m in (1, 3, 2):
                j = (z + m) % 4
                arrived(0, j, odd, a2_rs.at[j, odd])

            @pl.when(2 * core + odd != y)
            def _():
                for j in range(4):
                    arrived(1, j, odd, b2_rs.at[j, odd])

    def drain():
        for j in range(4):
            @pl.when(jnp.logical_not(jnp.logical_and(own_part, z == j)))
            def _():
                first(j).wait_send()
        for n in range(1, 4):
            for odd in range(2):
                a2(odd, n).wait_send()

        @pl.when(holder)
        def _():
            for n in range(1, 4):
                a1(n).wait_send()
                b1(n).wait_send()
                for m in range(4):
                    b2(m, n).wait_send()

    for k in range(NBLK):
        total = memory(k, panel_now if k == 0 else panel_next)
        rhs = total if k == 0 else total + held[...]
        if k == 0:
            inv_load.wait()
        solved = dot(inv_ref[k], rhs, HIGHEST)
        held[...] = solved
        self_energy(k)
        if k + 1 < NBLK:
            sigma_out[...] = sig[...].astype(bf16)
            exchange()
            relay()
        rows_ref[k] = held[...].T
        sigma_ref[k] = sig[...].T.astype(bf16)
        if k + 1 < NBLK:
            settle()
    drain()


def per_device(hist_green, sigma_panel, step_operator, coupling, pair_index):
    inverse = invert(step_operator)
    pairs = pair_index.reshape(3 * Q, PAIRS)
    depth = sigma_panel.shape[0]
    anywhere = pl.BlockSpec(memory_space=pl.ANY)
    vmem = pl.BlockSpec(memory_space=pltpu.VMEM)
    dma = pltpu.SemaphoreType.DMA
    rows, sigma = pl.pallas_call(
        window_kernel,
        out_shape=(
            jax.ShapeDtypeStruct((NBLK, LANES, WIDE), f32),
            jax.ShapeDtypeStruct((NBLK, LANES, WIDE), bf16),
        ),
        in_specs=[anywhere, anywhere, anywhere, vmem, vmem],
        out_specs=(vmem, vmem),
        scratch_shapes=[
            pltpu.VMEM((TILES, 3 * Q, 8, LANES), i32),
            pltpu.VMEM((TILES, Q, 8, LANES), f32),
            pltpu.VMEM((8, depth, 2 * LANES), bf16),
            pltpu.VMEM((depth, WIDE), bf16),
            pltpu.VMEM((WIDE, depth), bf16),
            pltpu.VMEM((WIDE, depth), bf16),
            pltpu.VMEM((NBLK, WIDE, WIDE), f32),
            pltpu.VMEM((WIDE, LANES), f32),
            pltpu.VMEM((4, 64, LANES), i32),
            pltpu.VMEM((TILES, 4, 8, LANES), i32),
            pltpu.VMEM((4, TILES, 16, LANES), f32),
            pltpu.VMEM((WIDE, LANES), f32),
            pltpu.VMEM((WIDE, LANES), bf16),
            pltpu.VMEM((NBLK, 4, WIDE, LANES), f32),
            pltpu.VMEM((NBLK, 4, WIDE, LANES), f32),
            pltpu.VMEM((NBLK, 4, WIDE, LANES), f32),
            pltpu.VMEM((NBLK, 3, HALF, LANES), i32),
            pltpu.VMEM((NBLK, 3, HALF, LANES), i32),
            pltpu.VMEM((NBLK, 3, 8, LANES), f32),
            pltpu.VMEM((NBLK, 3, 8, LANES), f32),
            dma((8, 2)), dma((2,)),
            dma((NBLK, 4)), dma((NBLK, 4)),
            dma((NBLK, 3)), dma((NBLK, 3)),
            dma((NBLK, 3)), dma((NBLK, 3)),
            dma((4,)), dma((8,)), dma(()),
            dma((3,)), dma((2,)), dma((2, 3)), dma((4, 2)),
            dma((3,)), dma((4,)), dma((4, 3)), dma((4, 2)),
        ],
        compiler_params=pltpu.CompilerParams(
            collective_id=0, has_side_effects=True, vmem_limit_bytes=56 << 20
        ),
    )(hist_green, sigma_panel, inverse, pairs, coupling)
    return rows[:, None], sigma[:, None]


def solution(mesh):
    return jax.shard_map(
        per_device,
        mesh=mesh,
        in_specs=(P(None, "hist", "tsec"), P("hist", None), P(), P(), P()),
        out_specs=(P(None, "tsec", "hist", None), P(None, "tsec", "hist", None)),
        check_vma=False,
    )
```

time: 217 us -> 95.9 us (0.44)
  the two profiles are of different devices: /device:TPU:34 before, /device:TPU:1 now
where the time goes in v2:
time: 95.9 us; the launch traced here: 95.6 us
  Pallas kernels  88.8 us (93%)
  local copies, waits for them, and re-layouts  6.08 us (6%)
    pallas_call x1, Pallas kernels, per_device(): pl.pallas_call(window_kernel, out_shape=(jax.ShapeDtypeStruct((NBLK, LANE...  81.1 us
    pallas_call x1, Pallas kernels, invert(): pl.pallas_call(inverse_kernel, grid=(NBLK,), out_shape=jax.ShapeDtypeStru...  7.71 us
    unnamed x6, local copies, waits for them, and re-layouts  6.08 us

profile of v2, /device:TPU:1, one launch (start us, length us, event | category | flops | bytes accessed | tf_op | source)
XLA Modules:
  0.0 95.6 jit_solution(8680763629559250066)
XLA Ops:
  0.6 0.0 copy-start.1
  0.6 1.2 %copy-done.1 = f32[2,2,256,256]{3,2,1,0:T(8,128)S(1)} copy-done((f32[2,2,256,256]{3,2,1,0:T(8,128)S(1)}, f32[2,2,256,256]{3,2,1,0:T(8,128)}, u32[]{:S(2)}) %copy-start.1) | copy-done | bytes 1048600
  1.9 7.7 %shard_map.68.inv_hbm = f32[2,512,512]{2,1,0:T(8,128)S(1)} custom-call(f32[2,2,256,256]{3,2,1,0:T(8,128)S(1)} %copy-done.1), custom_call_target="tpu_custom_call" | custom-call | tf_op jit(solution)/shard_map/pallas_call | solution.py:69
  9.6 0.0 copy-start
  9.6 1.3 %copy-done = f32[2,512,512]{2,1,0:T(8,128)} copy-done((f32[2,512,512]{2,1,0:T(8,128)}, f32[2,512,512]{2,1,0:T(8,128)S(1)}, u32[]{:S(2)}) %copy-start) | copy-done | bytes 2097176
  10.9 81.1 %shard_map.69 = (f32[2,128,512]{2,1,0:T(8,128)}, bf16[2,128,512]{2,1,0:T(8,128)(2,1)}) custom-call(bf16[2,2048,1024]{2,1,0:T(8,128)(2,1)} %green_hbm.1, bf16[2048,512]{1,0:T(8,128)(2,1)} %panel_hbm.1, f32[2,512,512]{2,1,0:T(8,128)} %copy-done, s32[24,1024]{1,0:T(8,128)} %bitcast.9, f32[8,1024]{1,0:T(8,128)} %weight_ref.1), custom_call_target="tpu_custom_call" | custom-call | tf_op jit(solution)/shard_map/pallas_call | solution.py:448
  92.1 1.9 %copy.11 = f32[2,1,128,512]{3,2,1,0:T(8,128)} copy(f32[2,1,128,512]{3,2,1,0:T(8,128)} %bitcast.7) | data formatting | bytes 1048576
  93.9 1.7 %copy.12 = bf16[2,1,128,512]{3,2,1,0:T(8,128)(2,1)} copy(bf16[2,1,128,512]{3,2,1,0:T(8,128)(2,1)} %bitcast.8) | data formatting | bytes 524288
Async XLA Ops:
  0.6 1.2 %copy-start.1 = (f32[2,2,256,256]{3,2,1,0:T(8,128)S(1)}, f32[2,2,256,256]{3,2,1,0:T(8,128)}, u32[]{:S(2)}) copy-start(f32[2,2,256,256]{3,2,1,0:T(8,128)} %op_ref.1) | copy-start | bytes 3145732
  9.6 1.3 %copy-start = (f32[2,512,512]{2,1,0:T(8,128)}, f32[2,512,512]{2,1,0:T(8,128)S(1)}, u32[]{:S(2)}) copy-start(f32[2,512,512]{2,1,0:T(8,128)S(1)} %shard_map.68.inv_hbm) | copy-start | bytes 6291460

commit v3 on v2

v3 whole, which is shorter than its diff:
```python
import functools

import jax
import jax.numpy as jnp
from jax import lax
from jax.experimental import pallas as pl
from jax.experimental.pallas import tpu as pltpu
from jax.sharding import PartitionSpec as P

N = 32
B = 8
NBLK = 2
Q = 8
HALF = B * N
WIDE = 2 * HALF
LANES = 128
PAIRS = N * N
TILES = PAIRS // LANES
MESH = pl.DeviceIdType.MESH
f32, bf16, i32 = jnp.float32, jnp.bfloat16, jnp.int32
HIGHEST = lax.Precision.HIGHEST
PEAK = 32000.0


def dot(left, right, precision=None):
    return jnp.dot(left, right, preferred_element_type=f32, precision=precision)


def inverse_kernel(op_hbm, out_ref, a_ref, x_ref, r_ref, sem):
    load = pltpu.make_async_copy(op_hbm.at[lax.axis_index("hist") % 2], a_ref, sem)
    load.start()
    rows = lax.broadcasted_iota(i32, (HALF, HALF), 0)
    cols = lax.broadcasted_iota(i32, (HALF, HALF), 1)
    eye = jnp.where(rows == cols, 1.0, 0.0).astype(f32)
    load.wait()
    ar, ai = a_ref[0], a_ref[1]
    inv_row = 1.0 / jnp.sum(ar * eye, axis=0, keepdims=True)
    inv_col = 1.0 / jnp.sum(ar * eye, axis=1, keepdims=True)
    x_ref[:, :HALF] = inv_col * (eye + (eye - ar * inv_row))
    x_ref[:, HALF:] = inv_col * (-ai * inv_row)

    def product(left, right, precision):
        out = dot(left, right, precision)
        return out[:HALF, :HALF] - out[HALF:, HALF:], out[:HALF, HALF:] + out[HALF:, :HALF]

    def residual():
        re, im = product(a_ref[...].reshape(WIDE, HALF), x_ref[...], HIGHEST)
        re, im = eye - re, -im
        r_ref[:, :HALF] = re
        r_ref[:, HALF:] = im
        return jnp.max(jnp.sum(jnp.abs(re) + jnp.abs(im), axis=0, keepdims=True))

    def improve(precision):
        left = jnp.concatenate([x_ref[:, :HALF], x_ref[:, HALF:]], axis=0)
        re, im = product(left, r_ref[...], precision)
        x_ref[:, :HALF] = x_ref[:, :HALF] + re
        x_ref[:, HALF:] = x_ref[:, HALF:] + im

    def unfinished(carry):
        step, norm = carry
        return jnp.logical_and(step < 40, norm > 3e-3)

    def again(carry):
        improve(HIGHEST)
        return carry[0] + 1, residual()

    lax.while_loop(unfinished, again, (jnp.int32(0), residual()))
    improve(None)
    for part in range(2):
        value = x_ref[:, part * HALF : (part + 1) * HALF]
        high = value.astype(bf16)
        out_ref[part * HALF : (part + 1) * HALF] = high
        out_ref[WIDE + part * HALF : WIDE + (part + 1) * HALF] = (value - high.astype(f32)).astype(bf16)


def invert(step_operator):
    return pl.pallas_call(
        inverse_kernel,
        out_shape=jax.ShapeDtypeStruct((2 * WIDE, HALF), bf16),
        in_specs=[pl.BlockSpec(memory_space=pl.ANY)],
        out_specs=pl.BlockSpec(memory_space=pltpu.VMEM),
        scratch_shapes=[
            pltpu.VMEM((2, HALF, HALF), f32),
            pltpu.VMEM((HALF, WIDE), f32),
            pltpu.VMEM((HALF, WIDE), f32),
            pltpu.SemaphoreType.DMA(()),
        ],
        compiler_params=pltpu.CompilerParams(vmem_limit_bytes=32 << 20),
    )(step_operator)


def window_kernel(
    green_hbm, panel_hbm, inv_in, pair_ref, weight_ref,
    rows_ref, sigma_ref,
    pair_wide, weight_wide,
    green, panel_raw, panel_now, panel_next, inv_ref, held, field, packed, spread, wide, half_sig, sig, sigma_out,
    sib_send, sib_recv, sums, msg_send, msg_recv, unit_send, unit_recv,
    load_sem, in_sem, inv_ss, inv_rs, sib_ss, sib_rs, msg_ss, msg_rs, unit_ss, unit_rs,
    st_ss, st_rs, st_ls, a1_ss, a1_rs, a2_ss, a2_rs, b1_ss, b1_rs, b2_ss, b2_rs,
):
    hist, tsec = lax.axis_index("hist"), lax.axis_index("tsec")
    chip, core = hist // 2, hist % 2
    z, y = tsec // 4, tsec % 4
    sibling = chip * 2 + 1 - core
    holder = core == y // 2
    depth = panel_now.shape[1]

    def at_chip(o, which):
        return ((chip + o) % 4) * 2 + which

    def loads(d):
        lanes = pl.ds(pl.multiple_of(d * LANES, LANES), LANES)
        return [
            pltpu.make_async_copy(
                green_hbm.at[part, :, lanes],
                green.at[d, :, pl.ds(part * LANES, LANES)],
                load_sem.at[d, part],
            )
            for part in range(2)
        ]

    panel_load = pltpu.make_async_copy(panel_hbm, panel_raw, in_sem.at[0])
    inv_keep = pltpu.make_async_copy(inv_in, inv_ref.at[core], in_sem.at[1])
    panel_load.start()
    for o in (2, 1, 3, 0):
        for d in (at_chip(o, 1 - core), at_chip(o, core)):
            for copy in loads(d):
                copy.start()
    inv_keep.start()

    barrier = pltpu.get_barrier_semaphore()

    def greet(h, t):
        pl.semaphore_signal(barrier, inc=1, device_id={"hist": h, "tsec": t}, device_id_type=MESH)

    greet(sibling, tsec)
    for o in range(1, 4):
        greet(at_chip(o, core), tsec)
        greet(hist, z * 4 + (y + o) % 4)
        greet(hist, ((z + o) % 4) * 4 + y)
    for h in range(8):
        @pl.when(jnp.logical_and(holder, jnp.logical_or(hist != h, z != chip)))
        def _():
            greet(h, chip * 4 + y)

    for j in range(TILES):
        lanes = slice(j * LANES, (j + 1) * LANES)
        for r in range(3 * Q):
            pair_wide[j, r] = jnp.broadcast_to(pair_ref[r : r + 1, lanes], (8, LANES))
        for r in range(Q):
            weight_wide[j, r] = jnp.broadcast_to(weight_ref[r : r + 1, lanes], (8, LANES))

    panel_load.wait()
    for r in range(depth // HALF):
        panel_now[:, r * HALF : (r + 1) * HALF] = panel_raw[r * HALF : (r + 1) * HALF, :].T
    own_part = hist == 2 * z + y // 2
    is_last = jnp.where(hist == 7, 1.0, 0.0).astype(f32)

    def remote(src, dst, ss, rs, h, t):
        return pltpu.make_async_remote_copy(
            src_ref=src, dst_ref=dst, send_sem=ss, recv_sem=rs,
            device_id={"hist": h, "tsec": t}, device_id_type=MESH,
        )

    inv_give = remote(inv_in, inv_ref.at[core], inv_ss, inv_rs, sibling, tsec)
    inv_take = remote(inv_in, inv_ref.at[1 - core], inv_ss, inv_rs, sibling, tsec)

    def memory(run):
        k = min(run, 1)
        count = WIDE if run == 0 else HALF
        half = count // 2
        base = HALF if run == 2 else 0
        upper, lower = pl.ds(base, half), pl.ds(base + half, half)
        whole, msg_rows = pl.ds(base, count), pl.ds(base // 2, half)

        def chunk(d):
            left = panel_now[...] if run == 0 else panel_next[base : base + count, :]
            out = dot(left, green[d])
            re = out[:half, :LANES] - out[half:, LANES:]
            im = out[half:, :LANES] + out[:half, LANES:]
            if k == 0:
                tail = green[d, green.shape[1] - HALF :, :].astype(f32) * is_last
                re, im = re + tail[:, :LANES], im + tail[:, LANES:]
            return re, im

        def swap(i):
            return remote(
                sib_send.at[k, i, whole], sib_recv.at[k, i, whole], sib_ss.at[run, i], sib_rs.at[run, i], sibling, tsec
            )

        def messages(o):
            there, n = at_chip(o, core), o - 1
            return (
                remote(msg_send.at[k, n, msg_rows], msg_recv.at[k, n, msg_rows], msg_ss.at[run, n], msg_rs.at[run, n], there, tsec),
                remote(unit_send.at[run, n], unit_recv.at[run, n], unit_ss.at[run, n], unit_rs.at[run, n], there, tsec),
            )

        def offset(i):
            return jnp.where(i == 0, 2, jnp.where(i == 1, 1, jnp.where(i == 2, 3, 0)))

        def finish(last):
            swap(last).wait()
            o = offset(last)
            re = sums[k, last, upper] + sib_recv[k, last, upper]
            im = sums[k, last, lower] + sib_recv[k, last, lower]
            peak = jnp.maximum(jnp.max(jnp.maximum(jnp.abs(re), jnp.abs(im))), 1e-30)
            scale = PEAK / peak
            high = jnp.round(re * scale).astype(i32)
            low = jnp.round(im * scale).astype(i32)
            msg_send[k, o - 1, msg_rows] = lax.shift_left(high, 16) | (low & 0xFFFF)
            unit_send[run, o - 1] = jnp.full((8, LANES), 1.0, f32) * (peak / PEAK)
            for copy in messages(o):
                copy.start()

        late = 1 if k == 0 else 0

        def step(i, carry):
            far = at_chip(offset(i), 1 - core)
            if k == 0:
                for copy in loads(far):
                    copy.wait()
            re, im = chunk(far)
            sib_send[k, i, upper] = re
            sib_send[k, i, lower] = im
            if k == 0:
                @pl.when(i == 1)
                def _():
                    pl.semaphore_wait(barrier, jnp.where(own_part, 13, 14))
                    swap(0).start()

                @pl.when(i >= 1)
                def _():
                    swap(i).start()

                @pl.when(i == 3)
                def _():
                    inv_give.start()
            else:
                swap(i).start()

            @pl.when(i > late)
            def _():
                finish(i - 1 - late)

            near = at_chip(offset(i), core)
            if k == 0:
                for copy in loads(near):
                    copy.wait()
            re, im = chunk(near)
            sums[k, i, upper] = re
            sums[k, i, lower] = im
            return carry

        lax.fori_loop(0, 4, step, 0)
        for last in range(3 - late, 3):
            finish(last)
        swap(3).wait()

        def collect():
            re = sums[k, 3, upper] + sib_recv[k, 3, upper]
            im = sums[k, 3, lower] + sib_recv[k, 3, lower]
            for o in (1, 3, 2):
                for copy in messages(o):
                    copy.wait()
                both = msg_recv[k, o - 1, msg_rows]
                unit = unit_recv[run, o - 1, :1, :1]
                re = re + lax.shift_right_arithmetic(both, 16).astype(f32) * unit
                im = im + lax.shift_right_arithmetic(lax.shift_left(both, 16), 16).astype(f32) * unit
            return re, im

        return collect

    def regroup(count, pick, store):
        lane_group = lax.broadcasted_iota(i32, (count, LANES), 1) // N
        for s in range(4):
            value = None
            for a in range(4):
                moved = pick(a)
                if a != s:
                    moved = pltpu.roll(moved, (N * (a - s)) % LANES, 1)
                value = moved if value is None else jnp.where(lane_group == a, moved, value)
            store(s, value)

    def self_energy():
        peak = jnp.maximum(jnp.max(jnp.abs(held[...])), 1e-30)
        scale, unit = PEAK / peak, peak / PEAK

        def store_field(s, value):
            whole = jnp.round(value * scale).astype(i32)
            both = lax.shift_left(whole[:64], 16) | (whole[64:] & 0xFFFF)
            field[s] = both
        regroup(LANES, lambda a: held[pl.ds(a, LANES, stride=4), :], store_field)
        for j in range(TILES):
            for s in range(4):
                packed[j, s] = field[s, pl.ds(j, 8, stride=TILES), :]

        def tile(j, carry):
            def term(q, acc):
                values = []
                for f in range(3):
                    pair = pair_wide[j, f * Q + q]
                    low, high = pair & (LANES - 1), lax.shift_right_logical(pair, 7)
                    masks = [high == n for n in range(1, TILES)]
                    parts = []
                    for s in range(4):
                        found = jnp.take_along_axis(packed[0, s], low, axis=1)
                        for n in range(1, TILES):
                            found = jnp.where(masks[n - 1], jnp.take_along_axis(packed[n, s], low, axis=1), found)
                        parts.append((
                            lax.shift_right_arithmetic(found, 16).astype(f32),
                            lax.shift_right_arithmetic(lax.shift_left(found, 16), 16).astype(f32),
                        ))
                    values.append(parts)
                weight = weight_wide[j, q]
                result = []
                for s in range(4):
                    (ar, ai), (br, bi), (cr, ci) = values[0][s], values[1][s], values[2][s]
                    pr, pi = ar * br - ai * bi, ar * bi + ai * br
                    result.append(acc[2 * s] + weight * (pr * cr + pi * ci))
                    result.append(acc[2 * s + 1] + weight * (pi * cr - pr * ci))
                return tuple(result)

            acc = lax.fori_loop(0, Q, term, tuple(jnp.zeros((8, LANES), f32) for _ in range(8)), unroll=4)
            for s in range(4):
                for part in range(2):
                    spread[s, j, part * 8 : part * 8 + 8, :] = acc[2 * s + part] * (unit * unit * unit)
            return carry

        def tiles(start, stop):
            lax.fori_loop(start, stop, tile, 0)

        def store_piece(a, value):
            half_sig[pl.ds(a, 64, stride=4), :] = value

        def collect(p, share):
            for s in range(4):
                for jj in range(4):
                    for part in range(2):
                        wide[s, pl.ds(part * 32 + jj, 8, stride=4), :] = spread[s, p * 4 + jj, part * 8 : part * 8 + 8, :]
            regroup(64, lambda s: wide[s], store_piece)
            if share:
                sigma_out[p * HALF : (p + 1) * HALF] = half_sig[...].astype(bf16)
            for n in range(16):
                sig[n * N + p * 16 : n * N + p * 16 + 16] = half_sig[n * 16 : n * 16 + 16]

        return tiles, collect

    def first(p, j):
        slot = pl.ds(pl.multiple_of((y % 2) * 1024 + hist * LANES, LANES), LANES)
        rows = pl.ds(p * HALF + j * 64, 64)
        return remote(
            sigma_out.at[rows], panel_next.at[rows, slot], st_ss.at[p, j], st_rs.at[p, hist], 2 * z + y // 2, 4 * j + y
        )

    def first_here(p, j):
        slot = pl.ds(pl.multiple_of((y % 2) * 1024 + hist * LANES, LANES), LANES)
        rows = pl.ds(p * HALF + j * 64, 64)
        return pltpu.make_async_copy(sigma_out.at[rows], panel_next.at[rows, slot], st_ls.at[p])

    def piece(p, second, j, odd):
        rows = pl.ds(pl.multiple_of(p * HALF + j * 64 + second * 32, 32), 32)
        return panel_next.at[rows, pl.ds(pl.multiple_of(odd * 1024, 1024), 1024)]

    def pass_on(p, second, j, odd, ss, rs, t):
        return remote(piece(p, second, j, odd), piece(p, second, j, odd), ss, rs, hist, t)

    def along_y(n):
        return z * 4 + (y + n) % 4

    def along_z(n):
        return ((z + n) % 4) * 4 + y

    def a1(p, n):
        return pass_on(p, 0, z, y % 2, a1_ss.at[p, n - 1], a1_rs.at[p, y % 2], along_y(n))

    def b1(p, n):
        return pass_on(p, 1, z, y % 2, b1_ss.at[p, n - 1], b1_rs.at[p, z], along_z(n))

    def a2(p, odd, n):
        return pass_on(p, 0, z, odd, a2_ss.at[p, odd, n - 1], a2_rs.at[p, z, odd], along_z(n))

    def b2(p, m, n):
        j = (z + m) % 4
        return pass_on(p, 1, j, y % 2, b2_ss.at[p, m, n - 1], b2_rs.at[p, j, y % 2], along_y(n))

    def exchange(p):
        for j in range(4):
            here = jnp.logical_and(own_part, z == j)

            @pl.when(jnp.logical_not(here))
            def _():
                first(p, j).start()

            @pl.when(here)
            def _():
                first_here(p, j).start()

    def arrived(p, second, j, odd, rs):
        pass_on(p, second, j, odd, a1_ss.at[p, 0], rs, along_y(1)).wait_recv()

    def relay_first(p):
        @pl.when(holder)
        def _():
            for h in range(8):
                slot = pl.ds(pl.multiple_of((y % 2) * 1024 + h * LANES, LANES), LANES)
                rows = pl.ds(pl.multiple_of(p * HALF + z * 64, 64), 64)

                @pl.when(jnp.logical_or(hist != h, z != chip))
                def _():
                    remote(
                        sigma_out.at[pl.ds(0, 64)], panel_next.at[rows, slot], st_ss.at[p, 0], st_rs.at[p, h], sibling, tsec
                    ).wait_recv()

            for j in range(4):
                @pl.when(jnp.logical_and(own_part, z == j))
                def _():
                    first_here(p, j).wait()

            for n in (2, 1, 3):
                a1(p, n).start()
                b1(p, n).start()
            for n in (2, 1, 3):
                a2(p, y % 2, n).start()
                b2(p, 0, n).start()

    def relay_second(p):
        for odd in range(2):
            @pl.when(2 * core + odd != y)
            def _():
                arrived(p, 0, z, odd, a1_rs.at[p, odd])
                for n in (2, 1, 3):
                    a2(p, odd, n).start()

        @pl.when(holder)
        def _():
            for m in (1, 3, 2):
                j = (z + m) % 4
                arrived(p, 1, j, y % 2, b1_rs.at[p, j])
                for n in (2, 1, 3):
                    b2(p, m, n).start()

    def settle(p):
        for odd in range(2):
            for m in (1, 3, 2):
                j = (z + m) % 4
                arrived(p, 0, j, odd, a2_rs.at[p, j, odd])

            @pl.when(2 * core + odd != y)
            def _():
                for j in range(4):
                    arrived(p, 1, j, odd, b2_rs.at[p, j, odd])

    def drain(p):
        for j in range(4):
            @pl.when(jnp.logical_not(jnp.logical_and(own_part, z == j)))
            def _():
                first(p, j).wait_send()
        for n in range(1, 4):
            for odd in range(2):
                a2(p, odd, n).wait_send()

        @pl.when(holder)
        def _():
            for n in range(1, 4):
                a1(p, n).wait_send()
                b1(p, n).wait_send()
                for m in range(4):
                    b2(p, m, n).wait_send()

    def solve(k, rhs):
        both = jnp.concatenate([rhs[:HALF], rhs[HALF:]], axis=1)
        high = both.astype(bf16)
        low = (both - high.astype(f32)).astype(bf16)
        out = dot(inv_ref[k], high)
        out = out[:WIDE] + out[WIDE:] + dot(inv_ref[k, :WIDE], low)
        held[:HALF] = out[:HALF, :LANES] - out[HALF:, LANES:]
        held[HALF:] = out[HALF:, :LANES] + out[:HALF, LANES:]

    re, im = memory(0)()
    inv_keep.wait()
    inv_take.wait_recv()
    solve(0, jnp.concatenate([re, im], axis=0))
    tiles, collect = self_energy()
    tiles(0, 4)
    collect(0, True)
    exchange(0)
    tiles(4, 6)
    relay_first(0)
    tiles(6, 8)
    collect(1, True)
    exchange(1)
    relay_second(0)
    rows_ref[0] = held[...].T
    sigma_ref[0] = sig[...].T.astype(bf16)
    relay_first(1)
    relay_second(1)
    settle(0)
    results = [memory(1)]
    settle(1)
    results.append(memory(2))
    for p in range(2):
        re, im = results[p]()
        for n in range(8):
            for part, value in enumerate((re, im)):
                at = part * HALF + n * N + p * 16
                held[at : at + 16] = held[at : at + 16] + value[n * 16 : n * 16 + 16]
    solve(1, held[...])
    tiles, collect = self_energy()
    rows_ref[1] = held[...].T
    tiles(0, 8)
    collect(0, False)
    collect(1, False)
    sigma_ref[1] = sig[...].T.astype(bf16)
    inv_give.wait_send()
    for p in range(2):
        drain(p)


def per_device(hist_green, sigma_panel, step_operator, coupling, pair_index):
    inverse = invert(step_operator)
    pairs = pair_index.reshape(3 * Q, PAIRS)
    depth = sigma_panel.shape[0]
    anywhere = pl.BlockSpec(memory_space=pl.ANY)
    vmem = pl.BlockSpec(memory_space=pltpu.VMEM)
    dma = pltpu.SemaphoreType.DMA
    rows, sigma = pl.pallas_call(
        window_kernel,
        out_shape=(
            jax.ShapeDtypeStruct((NBLK, LANES, WIDE), f32),
            jax.ShapeDtypeStruct((NBLK, LANES, WIDE), bf16),
        ),
        in_specs=[anywhere, anywhere, vmem, vmem, vmem],
        out_specs=(vmem, vmem),
        scratch_shapes=[
            pltpu.VMEM((TILES, 3 * Q, 8, LANES), i32),
            pltpu.VMEM((TILES, Q, 8, LANES), f32),
            pltpu.VMEM((8, depth, 2 * LANES), bf16),
            pltpu.VMEM((depth, WIDE), bf16),
            pltpu.VMEM((WIDE, depth), bf16),
            pltpu.VMEM((WIDE, depth), bf16),
            pltpu.VMEM((NBLK, 2 * WIDE, HALF), bf16),
            pltpu.VMEM((WIDE, LANES), f32),
            pltpu.VMEM((4, 64, LANES), i32),
            pltpu.VMEM((TILES, 4, 8, LANES), i32),
            pltpu.VMEM((4, TILES, 16, LANES), f32),
            pltpu.VMEM((4, 64, LANES), f32),
            pltpu.VMEM((HALF, LANES), f32),
            pltpu.VMEM((WIDE, LANES), f32),
            pltpu.VMEM((WIDE, LANES), bf16),
            pltpu.VMEM((NBLK, 4, WIDE, LANES), f32),
            pltpu.VMEM((NBLK, 4, WIDE, LANES), f32),
            pltpu.VMEM((NBLK, 4, WIDE, LANES), f32),
            pltpu.VMEM((NBLK, 3, HALF, LANES), i32),
            pltpu.VMEM((NBLK, 3, HALF, LANES), i32),
            pltpu.VMEM((3, 3, 8, LANES), f32),
            pltpu.VMEM((3, 3, 8, LANES), f32),
            dma((8, 2)), dma((2,)), dma(()), dma(()),
            dma((3, 4)), dma((3, 4)),
            dma((3, 3)), dma((3, 3)),
            dma((3, 3)), dma((3, 3)),
            dma((2, 4)), dma((2, 8)), dma((2,)),
            dma((2, 3)), dma((2, 2)), dma((2, 2, 3)), dma((2, 4, 2)),
            dma((2, 3)), dma((2, 4)), dma((2, 4, 3)), dma((2, 4, 2)),
        ],
        compiler_params=pltpu.CompilerParams(
            collective_id=0, has_side_effects=True, vmem_limit_bytes=56 << 20
        ),
    )(hist_green, sigma_panel, inverse, pairs, coupling)
    return rows[:, None], sigma[:, None]


def solution(mesh):
    return jax.shard_map(
        per_device,
        mesh=mesh,
        in_specs=(P(None, "hist", "tsec"), P("hist", None), P(), P(), P()),
        out_specs=(P(None, "tsec", "hist", None), P(None, "tsec", "hist", None)),
        check_vma=False,
    )
```

time: 95.9 us -> 87.4 us (0.911)
  Pallas kernels: 88.8 us -> 81 us
    pallas_call x1, Pallas kernels: 81.1 us -> 75.6 us  [per_device(): pl.pallas_call(window_kernel, out_shape=(jax.ShapeDtypeStruct((NBLK, LANE...]
    pallas_call x1, Pallas kernels: 7.71 us -> 5.38 us  [invert(): pl.pallas_call(inverse_kernel, out_shape=jax.ShapeDtypeStruct((2 * WIDE,...]
where the time goes in v3:
time: 87.4 us; the launch traced here: 87.2 us
  Pallas kernels  81 us (93%)
  local copies, waits for them, and re-layouts  5.54 us (6%)
    pallas_call x1, Pallas kernels, per_device(): pl.pallas_call(window_kernel, out_shape=(jax.ShapeDtypeStruct((NBLK, LANE...  75.6 us
    unnamed x6, local copies, waits for them, and re-layouts  5.54 us
    pallas_call x1, Pallas kernels, invert(): pl.pallas_call(inverse_kernel, out_shape=jax.ShapeDtypeStruct((2 * WIDE,...  5.38 us

profile of v3, /device:TPU:1, one launch (start us, length us, event | category | flops | bytes accessed | tf_op | source)
XLA Modules:
  0.0 87.2 jit_solution(2240634634464594477)
XLA Ops:
  0.6 0.0 copy-start.1
  0.6 1.2 %copy-done.1 = f32[2,2,256,256]{3,2,1,0:T(8,128)S(1)} copy-done((f32[2,2,256,256]{3,2,1,0:T(8,128)S(1)}, f32[2,2,256,256]{3,2,1,0:T(8,128)}, u32[]{:S(2)}) %copy-start.1) | copy-done | bytes 1048600
  1.9 5.4 %shard_map.68.inv_in = bf16[1024,256]{1,0:T(8,128)(2,1)S(1)} custom-call(f32[2,2,256,256]{3,2,1,0:T(8,128)S(1)} %copy-done.1), custom_call_target="tpu_custom_call" | custom-call | tf_op jit(solution)/shard_map/pallas_call | solution.py:77
  7.2 0.0 copy-start
  7.3 0.8 copy-done
  8.0 75.6 %shard_map.69 = (f32[2,128,512]{2,1,0:T(8,128)}, bf16[2,128,512]{2,1,0:T(8,128)(2,1)}) custom-call(bf16[2,2048,1024]{2,1,0:T(8,128)(2,1)} %green_hbm.1, bf16[2048,512]{1,0:T(8,128)(2,1)} %panel_hbm.1, bf16[1024,256]{1,0:T(8,128)(2,1)} %copy-done, s32[24,1024]{1,0:T(8,128)} %bitcast.9, f32[8,1024]{1,0:T(8,128)} %weight_ref.1), custom_call_target="tpu_custom_call" | custom-call | tf_op jit(solution)/shard_map/pallas_call | solution.py:526
  83.6 1.9 %copy.11 = f32[2,1,128,512]{3,2,1,0:T(8,128)} copy(f32[2,1,128,512]{3,2,1,0:T(8,128)} %bitcast.7) | data formatting | bytes 1048576
  85.5 1.7 %copy.12 = bf16[2,1,128,512]{3,2,1,0:T(8,128)(2,1)} copy(bf16[2,1,128,512]{3,2,1,0:T(8,128)(2,1)} %bitcast.8) | data formatting | bytes 524288
Async XLA Ops:
  0.6 1.2 %copy-start.1 = (f32[2,2,256,256]{3,2,1,0:T(8,128)S(1)}, f32[2,2,256,256]{3,2,1,0:T(8,128)}, u32[]{:S(2)}) copy-start(f32[2,2,256,256]{3,2,1,0:T(8,128)} %op_hbm.1) | copy-start | bytes 3145732
  7.2 0.8 copy-start

commit v4 on v3

--- a/solution.py
+++ b/solution.py
@@ -26,13 +26,11 @@
     return jnp.dot(left, right, preferred_element_type=f32, precision=precision)
 
 
-def inverse_kernel(op_hbm, out_ref, a_ref, x_ref, r_ref, sem):
-    load = pltpu.make_async_copy(op_hbm.at[lax.axis_index("hist") % 2], a_ref, sem)
-    load.start()
+def prepare_kernel(op_ref, pair_ref, weight_ref, out_ref, pair_wide, weight_wide, x_ref, r_ref):
+    a_ref = op_ref.at[lax.axis_index("hist") % 2]
     rows = lax.broadcasted_iota(i32, (HALF, HALF), 0)
     cols = lax.broadcasted_iota(i32, (HALF, HALF), 1)
     eye = jnp.where(rows == cols, 1.0, 0.0).astype(f32)
-    load.wait()
     ar, ai = a_ref[0], a_ref[1]
     inv_row = 1.0 / jnp.sum(ar * eye, axis=0, keepdims=True)
     inv_col = 1.0 / jnp.sum(ar * eye, axis=1, keepdims=True)
@@ -71,29 +69,146 @@
         high = value.astype(bf16)
         out_ref[part * HALF : (part + 1) * HALF] = high
         out_ref[WIDE + part * HALF : WIDE + (part + 1) * HALF] = (value - high.astype(f32)).astype(bf16)
-
-
-def invert(step_operator):
+    for j in range(TILES):
+        lanes = slice(j * LANES, (j + 1) * LANES)
+        for r in range(3 * Q):
+            pair_wide[j, r] = jnp.broadcast_to(pair_ref[r : r + 1, lanes], (8, LANES))
+        for r in range(Q):
+            weight_wide[j, r] = jnp.broadcast_to(weight_ref[r : r + 1, lanes], (8, LANES))
+
+
+def prepare(step_operator, pairs, coupling):
+    vmem = pl.BlockSpec(memory_space=pltpu.VMEM)
     return pl.pallas_call(
-        inverse_kernel,
-        out_shape=jax.ShapeDtypeStruct((2 * WIDE, HALF), bf16),
-        in_specs=[pl.BlockSpec(memory_space=pl.ANY)],
-        out_specs=pl.BlockSpec(memory_space=pltpu.VMEM),
-        scratch_shapes=[
-            pltpu.VMEM((2, HALF, HALF), f32),
-            pltpu.VMEM((HALF, WIDE), f32),
-            pltpu.VMEM((HALF, WIDE), f32),
-            pltpu.SemaphoreType.DMA(()),
-        ],
+        prepare_kernel,
+        out_shape=(
+            jax.ShapeDtypeStruct((2 * WIDE, HALF), bf16),
+            jax.ShapeDtypeStruct((TILES, 3 * Q, 8, LANES), i32),
+            jax.ShapeDtypeStruct((TILES, Q, 8, LANES), f32),
+        ),
+        in_specs=[vmem] * 3,
+        out_specs=(vmem,) * 3,
+        scratch_shapes=[pltpu.VMEM((HALF, WIDE), f32), pltpu.VMEM((HALF, WIDE), f32)],
         compiler_params=pltpu.CompilerParams(vmem_limit_bytes=32 << 20),
-    )(step_operator)
+    )(step_operator, pairs, coupling)
+
+
+def regroup(count, pick, store):
+    lane_group = lax.broadcasted_iota(i32, (count, LANES), 1) // N
+    for s in range(4):
+        value = None
+        for a in range(4):
+            moved = pick(a)
+            if a != s:
+                moved = pltpu.roll(moved, (N * (a - s)) % LANES, 1)
+            value = moved if value is None else jnp.where(lane_group == a, moved, value)
+        store(s, value)
+
+
+def self_energy(held, sigma_out, pair_wide, weight_wide, field, packed, spread, wide, half_sig, sig):
+    peak = jnp.maximum(jnp.max(jnp.abs(held[...])), 1e-30)
+    scale, unit = PEAK / peak, peak / PEAK
+
+    def store_field(s, value):
+        whole = jnp.round(value * scale).astype(i32)
+        both = lax.shift_left(whole[:64], 16) | (whole[64:] & 0xFFFF)
+        field[s] = both
+    regroup(LANES, lambda a: held[pl.ds(a, LANES, stride=4), :], store_field)
+    for j in range(TILES):
+        for s in range(4):
+            packed[j, s] = field[s, pl.ds(j, 8, stride=TILES), :]
+
+    def tile(j, carry):
+        def term(q, acc):
+            values = []
+            for f in range(3):
+                pair = pair_wide[j, f * Q + q]
+                low, high = pair & (LANES - 1), lax.shift_right_logical(pair, 7)
+                masks = [high == n for n in range(1, TILES)]
+                parts = []
+                for s in range(4):
+                    found = jnp.take_along_axis(packed[0, s], low, axis=1)
+                    for n in range(1, TILES):
+                        found = jnp.where(masks[n - 1], jnp.take_along_axis(packed[n, s], low, axis=1), found)
+                    parts.append((
+                        lax.shift_right_arithmetic(found, 16).astype(f32),
+                        lax.shift_right_arithmetic(lax.shift_left(found, 16), 16).astype(f32),
+                    ))
+                values.append(parts)
+            weight = weight_wide[j, q]
+            result = []
+            for s in range(4):
+                (ar, ai), (br, bi), (cr, ci) = values[0][s], values[1][s], values[2][s]
+                pr, pi = ar * br - ai * bi, ar * bi + ai * br
+                result.append(acc[2 * s] + weight * (pr * cr + pi * ci))
+                result.append(acc[2 * s + 1] + weight * (pi * cr - pr * ci))
+            return tuple(result)
+
+        acc = lax.fori_loop(0, Q, term, tuple(jnp.zeros((8, LANES), f32) for _ in range(8)), unroll=8)
+        for s in range(4):
+            for part in range(2):
+                spread[s, j, part * 8 : part * 8 + 8, :] = acc[2 * s + part] * (unit * unit * unit)
+        return carry
+
+    def tiles(start, stop):
+        lax.fori_loop(start, stop, tile, 0)
+
+    def store_piece(a, value):
+        half_sig[pl.ds(a, 64, stride=4), :] = value
+
+    def collect(p, share):
+        for s in range(4):
+            for jj in range(4):
+                for part in range(2):
+                    wide[s, pl.ds(part * 32 + jj, 8, stride=4), :] = spread[s, p * 4 + jj, part * 8 : part * 8 + 8, :]
+        regroup(64, lambda s: wide[s], store_piece)
+        if share:
+            sigma_out[p * HALF : (p + 1) * HALF] = half_sig[...].astype(bf16)
+        for n in range(16):
+            sig[n * N + p * 16 : n * N + p * 16 + 16] = half_sig[n * 16 : n * 16 + 16]
+
+    return tiles, collect
+
+
+ENERGY_SCRATCH = [
+    pltpu.VMEM((4, 64, LANES), i32),
+    pltpu.VMEM((TILES, 4, 8, LANES), i32),
+    pltpu.VMEM((4, TILES, 16, LANES), f32),
+    pltpu.VMEM((4, 64, LANES), f32),
+    pltpu.VMEM((HALF, LANES), f32),
+    pltpu.VMEM((WIDE, LANES), f32),
+]
+
+
+def final_kernel(
+    rows_first, sigma_first, held, pair_wide, weight_wide, rows_ref, sigma_ref,
+    field, packed, spread, wide, half_sig, sig, rows_out, sigma_out, sems,
+):
+    copies = [
+        pltpu.make_async_copy(rows_first, rows_ref.at[0, 0], sems.at[0]),
+        pltpu.make_async_copy(sigma_first, sigma_ref.at[0, 0], sems.at[1]),
+        pltpu.make_async_copy(rows_out, rows_ref.at[1, 0], sems.at[2]),
+        pltpu.make_async_copy(sigma_out, sigma_ref.at[1, 0], sems.at[3]),
+    ]
+    copies[0].start()
+    copies[1].start()
+    rows_out[...] = held[...].T
+    copies[2].start()
+    tiles, collect = self_energy(held, None, pair_wide, weight_wide, field, packed, spread, wide, half_sig, sig)
+    tiles(0, 8)
+    collect(0, False)
+    collect(1, False)
+    sigma_out[...] = sig[...].T.astype(bf16)
+    copies[3].start()
+    for copy in copies:
+        copy.wait()
 
 
 def window_kernel(
-    green_hbm, panel_hbm, inv_in, pair_ref, weight_ref,
-    rows_ref, sigma_ref,
-    pair_wide, weight_wide,
-    green, panel_raw, panel_now, panel_next, inv_ref, held, field, packed, spread, wide, half_sig, sig, sigma_out,
+    green_hbm, panel_hbm, inv_in, pair_wide, weight_wide,
+    rows_ref, sigma_ref, last_ref,
+    field, packed, spread, wide, half_sig, sig,
+    green, panel_raw, panel_now, panel_next, inv_ref, held, sigma_out,
     sib_send, sib_recv, sums, msg_send, msg_recv, unit_send, unit_recv,
     load_sem, in_sem, inv_ss, inv_rs, sib_ss, sib_rs, msg_ss, msg_rs, unit_ss, unit_rs,
     st_ss, st_rs, st_ls, a1_ss, a1_rs, a2_ss, a2_rs, b1_ss, b1_rs, b2_ss, b2_rs,
@@ -142,13 +257,6 @@
         @pl.when(jnp.logical_and(holder, jnp.logical_or(hist != h, z != chip)))
         def _():
             greet(h, chip * 4 + y)
-
-    for j in range(TILES):
-        lanes = slice(j * LANES, (j + 1) * LANES)
-        for r in range(3 * Q):
-            pair_wide[j, r] = jnp.broadcast_to(pair_ref[r : r + 1, lanes], (8, LANES))
-        for r in range(Q):
-            weight_wide[j, r] = jnp.broadcast_to(weight_ref[r : r + 1, lanes], (8, LANES))
 
     panel_load.wait()
     for r in range(depth // HALF):
@@ -270,81 +378,6 @@
 
         return collect
 
-    def regroup(count, pick, store):
-        lane_group = lax.broadcasted_iota(i32, (count, LANES), 1) // N
-        for s in range(4):
-            value = None
-            for a in range(4):
-                moved = pick(a)
-                if a != s:
-                    moved = pltpu.roll(moved, (N * (a - s)) % LANES, 1)
-                value = moved if value is None else jnp.where(lane_group == a, moved, value)
-            store(s, value)
-
-    def self_energy():
-        peak = jnp.maximum(jnp.max(jnp.abs(held[...])), 1e-30)
-        scale, unit = PEAK / peak, peak / PEAK
-
-        def store_field(s, value):
-            whole = jnp.round(value * scale).astype(i32)
-            both = lax.shift_left(whole[:64], 16) | (whole[64:] & 0xFFFF)
-            field[s] = both
-        regroup(LANES, lambda a: held[pl.ds(a, LANES, stride=4), :], store_field)
-        for j in range(TILES):
-            for s in range(4):
-                packed[j, s] = field[s, pl.ds(j, 8, stride=TILES), :]
-
-        def tile(j, carry):
-            def term(q, acc):
-                values = []
-                for f in range(3):
-                    pair = pair_wide[j, f * Q + q]
-                    low, high = pair & (LANES - 1), lax.shift_right_logical(pair, 7)
-                    masks = [high == n for n in range(1, TILES)]
-                    parts = []
-                    for s in range(4):
-                        found = jnp.take_along_axis(packed[0, s], low, axis=1)
-                        for n in range(1, TILES):
-                            found = jnp.where(masks[n - 1], jnp.take_along_axis(packed[n, s], low, axis=1), found)
-                        parts.append((
-                            lax.shift_right_arithmetic(found, 16).astype(f32),
-                            lax.shift_right_arithmetic(lax.shift_left(found, 16), 16).astype(f32),
-                        ))
-                    values.append(parts)
-                weight = weight_wide[j, q]
-                result = []
-                for s in range(4):
-                    (ar, ai), (br, bi), (cr, ci) = values[0][s], values[1][s], values[2][s]
-                    pr, pi = ar * br - ai * bi, ar * bi + ai * br
-                    result.append(acc[2 * s] + weight * (pr * cr + pi * ci))
-                    result.append(acc[2 * s + 1] + weight * (pi * cr - pr * ci))
-                return tuple(result)
-
-            acc = lax.fori_loop(0, Q, term, tuple(jnp.zeros((8, LANES), f32) for _ in range(8)), unroll=4)
-            for s in range(4):
-                for part in range(2):
-                    spread[s, j, part * 8 : part * 8 + 8, :] = acc[2 * s + part] * (unit * unit * unit)
-            return carry
-
-        def tiles(start, stop):
-            lax.fori_loop(start, stop, tile, 0)
-
-        def store_piece(a, value):
-            half_sig[pl.ds(a, 64, stride=4), :] = value
-
-        def collect(p, share):
-            for s in range(4):
-                for jj in range(4):
-                    for part in range(2):
-                        wide[s, pl.ds(part * 32 + jj, 8, stride=4), :] = spread[s, p * 4 + jj, part * 8 : part * 8 + 8, :]
-            regroup(64, lambda s: wide[s], store_piece)
-            if share:
-                sigma_out[p * HALF : (p + 1) * HALF] = half_sig[...].astype(bf16)
-            for n in range(16):
-                sig[n * N + p * 16 : n * N + p * 16 + 16] = half_sig[n * 16 : n * 16 + 16]
-
-        return tiles, collect
-
     def first(p, j):
         slot = pl.ds(pl.multiple_of((y % 2) * 1024 + hist * LANES, LANES), LANES)
         rows = pl.ds(p * HALF + j * 64, 64)
@@ -480,7 +513,9 @@
     inv_keep.wait()
     inv_take.wait_recv()
     solve(0, jnp.concatenate([re, im], axis=0))
-    tiles, collect = self_energy()
+    tiles, collect = self_energy(
+        held, sigma_out, pair_wide, weight_wide, field, packed, spread, wide, half_sig, sig
+    )
     tiles(0, 4)
     collect(0, True)
     exchange(0)
@@ -490,8 +525,8 @@
     collect(1, True)
     exchange(1)
     relay_second(0)
-    rows_ref[0] = held[...].T
-    sigma_ref[0] = sig[...].T.astype(bf16)
+    rows_ref[...] = held[...].T
+    sigma_ref[...] = sig[...].T.astype(bf16)
     relay_first(1)
     relay_second(1)
     settle(0)
@@ -505,46 +540,33 @@
                 at = part * HALF + n * N + p * 16
                 held[at : at + 16] = held[at : at + 16] + value[n * 16 : n * 16 + 16]
     solve(1, held[...])
-    tiles, collect = self_energy()
-    rows_ref[1] = held[...].T
-    tiles(0, 8)
-    collect(0, False)
-    collect(1, False)
-    sigma_ref[1] = sig[...].T.astype(bf16)
+    last_ref[...] = held[...]
     inv_give.wait_send()
     for p in range(2):
         drain(p)
 
 
 def per_device(hist_green, sigma_panel, step_operator, coupling, pair_index):
-    inverse = invert(step_operator)
-    pairs = pair_index.reshape(3 * Q, PAIRS)
+    inverse, pairs, weights = prepare(step_operator, pair_index.reshape(3 * Q, PAIRS), coupling)
     depth = sigma_panel.shape[0]
     anywhere = pl.BlockSpec(memory_space=pl.ANY)
     vmem = pl.BlockSpec(memory_space=pltpu.VMEM)
     dma = pltpu.SemaphoreType.DMA
-    rows, sigma = pl.pallas_call(
+    rows_first, sigma_first, last = pl.pallas_call(
         window_kernel,
         out_shape=(
-            jax.ShapeDtypeStruct((NBLK, LANES, WIDE), f32),
-            jax.ShapeDtypeStruct((NBLK, LANES, WIDE), bf16),
+            jax.ShapeDtypeStruct((LANES, WIDE), f32),
+            jax.ShapeDtypeStruct((LANES, WIDE), bf16),
+            jax.ShapeDtypeStruct((WIDE, LANES), f32),
         ),
         in_specs=[anywhere, anywhere, vmem, vmem, vmem],
-        out_specs=(vmem, vmem),
-        scratch_shapes=[
-            pltpu.VMEM((TILES, 3 * Q, 8, LANES), i32),
-            pltpu.VMEM((TILES, Q, 8, LANES), f32),
+        out_specs=(vmem, vmem, vmem),
+        scratch_shapes=ENERGY_SCRATCH + [
             pltpu.VMEM((8, depth, 2 * LANES), bf16),
             pltpu.VMEM((depth, WIDE), bf16),
             pltpu.VMEM((WIDE, depth), bf16),
             pltpu.VMEM((WIDE, depth), bf16),
             pltpu.VMEM((NBLK, 2 * WIDE, HALF), bf16),
-            pltpu.VMEM((WIDE, LANES), f32),
-            pltpu.VMEM((4, 64, LANES), i32),
-            pltpu.VMEM((TILES, 4, 8, LANES), i32),
-            pltpu.VMEM((4, TILES, 16, LANES), f32),
-            pltpu.VMEM((4, 64, LANES), f32),
-            pltpu.VMEM((HALF, LANES), f32),
             pltpu.VMEM((WIDE, LANES), f32),
             pltpu.VMEM((WIDE, LANES), bf16),
             pltpu.VMEM((NBLK, 4, WIDE, LANES), f32),
@@ -563,10 +585,24 @@
             dma((2, 3)), dma((2, 4)), dma((2, 4, 3)), dma((2, 4, 2)),
         ],
         compiler_params=pltpu.CompilerParams(
-            collective_id=0, has_side_effects=True, vmem_limit_bytes=56 << 20
+            collective_id=0, has_side_effects=True, vmem_limit_bytes=50 << 20
         ),
-    )(hist_green, sigma_panel, inverse, pairs, coupling)
-    return rows[:, None], sigma[:, None]
+    )(hist_green, sigma_panel, inverse, pairs, weights)
+    return pl.pallas_call(
+        final_kernel,
+        out_shape=(
+            jax.ShapeDtypeStruct((NBLK, 1, LANES, WIDE), f32),
+            jax.ShapeDtypeStruct((NBLK, 1, LANES, WIDE), bf16),
+        ),
+        in_specs=[anywhere, anywhere, vmem, vmem, vmem],
+        out_specs=(anywhere, anywhere),
+        scratch_shapes=ENERGY_SCRATCH + [
+            pltpu.VMEM((LANES, WIDE), f32),
+            pltpu.VMEM((LANES, WIDE), bf16),
+            dma((4,)),
+        ],
+        compiler_params=pltpu.CompilerParams(vmem_limit_bytes=24 << 20),
+    )(rows_first, sigma_first, last, pairs, weights)
 
 
 def solution(mesh):

time: 87.4 us -> 83.3 us (0.953)
  local copies, waits for them, and re-layouts: 5.54 us -> 2.87 us
  Pallas kernels: 81 us -> 79.4 us
    unnamed x6, local copies, waits for them, and re-layouts: 5.54 us -> 2.87 us
    pallas_call x2 -> x3, Pallas kernels: 81 us -> 79.4 us  [the longest x1 64.7 us: per_device(): pl.pallas_call(window_kernel, out_shape=(jax.ShapeDtypeStruct((LANES, WID...]
where the time goes in v4:
time: 83.3 us; the launch traced here: 83.1 us
  Pallas kernels  79.4 us (95%)
  local copies, waits for them, and re-layouts  2.87 us (3%)
    pallas_call x1, Pallas kernels, per_device(): pl.pallas_call(window_kernel, out_shape=(jax.ShapeDtypeStruct((LANES, WID...  64.7 us
    pallas_call x1, Pallas kernels, per_device(): pl.pallas_call(final_kernel, out_shape=(jax.ShapeDtypeStruct((NBLK, 1, LA...  9.31 us
    pallas_call x1, Pallas kernels, prepare(): pl.pallas_call(prepare_kernel, out_shape=(jax.ShapeDtypeStruct((2 * WIDE,...  5.37 us
    unnamed x6, local copies, waits for them, and re-layouts  2.87 us

profile of v4, /device:TPU:1, one launch (start us, length us, event | category | flops | bytes accessed | tf_op | source)
XLA Modules:
  0.0 83.1 jit_solution(17145853261576691349)
XLA Ops:
  0.6 0.0 copy-start
  0.6 1.2 %copy-done = f32[2,2,256,256]{3,2,1,0:T(8,128)S(1)} copy-done((f32[2,2,256,256]{3,2,1,0:T(8,128)S(1)}, f32[2,2,256,256]{3,2,1,0:T(8,128)}, u32[]{:S(2)}) %copy-start) | copy-done | bytes 1048600
  1.9 0.0 copy-start.1
  1.9 0.9 %copy-done.1 = s32[3,8,1024]{2,1,0:T(8,128)S(1)} copy-done((s32[3,8,1024]{2,1,0:T(8,128)S(1)}, s32[3,8,1024]{2,1,0:T(8,128)}, u32[]{:S(2)}) %copy-start.1) | copy-done | bytes 98328
  2.7 0.0 copy-start.2
  2.8 0.8 copy-done.2
  3.5 5.4 %shard_map.68 = (bf16[1024,256]{1,0:T(8,128)(2,1)S(1)}, s32[8,24,8,128]{3,2,1,0:T(8,128)S(1)}, f32[8,8,8,128]{3,2,1,0:T(8,128)S(1)}) custom-call(f32[2,2,256,256]{3,2,1,0:T(8,128)S(1)} %copy-done, s32[24,1024]{1,0:T(8,128)S(1)} %bitcast.1, f32[8,1024]{1,0:T(8,128)S(1)} %copy-done.2), custom_call_target="tpu_custom_call" | custom-call | tf_op jit(solution)/shard_map/pallas_call | solution.py:82
  8.9 64.7 %shard_map.69 = (f32[128,512]{1,0:T(8,128)S(1)}, bf16[128,512]{1,0:T(8,128)(2,1)S(1)}, f32[512,128]{1,0:T(8,128)S(1)}) custom-call(bf16[2,2048,1024]{2,1,0:T(8,128)(2,1)} %green_hbm.1, bf16[2048,512]{1,0:T(8,128)(2,1)} %panel_hbm.1, bf16[1024,256]{1,0:T(8,128)(2,1)S(1)} %get-tuple-element.8.inv_in, s32[8,24,8,128]{3,2,1,0:T(8,128)S(1)} %get-tuple-element.9.pair_wide, ...), custom_call_target="tpu_custom_call" | custom-call | tf_op jit(solution)/shard_map/pallas_call | solution.py:555
  73.6 9.3 %shard_map.70 = (f32[2,1,128,512]{3,2,1,0:T(8,128)}, bf16[2,1,128,512]{3,2,1,0:T(8,128)(2,1)}) custom-call(f32[128,512]{1,0:T(8,128)S(1)} %get-tuple-element.11.rows_first, bf16[128,512]{1,0:T(8,128)(2,1)S(1)} %get-tuple-element.12.sigma_first, f32[512,128]{1,0:T(8,128)S(1)} %get-tuple-element.13.held, s32[8,24,8,128]{3,2,1,0:T(8,128)S(1)} %get-tuple-element.9.pair_wide, ...), custom_call_target="tpu_custom_call" | custom-call | tf_op jit(solution)/shard_map/pallas_call | solution.py:591
Async XLA Ops:
  0.6 1.2 %copy-start = (f32[2,2,256,256]{3,2,1,0:T(8,128)S(1)}, f32[2,2,256,256]{3,2,1,0:T(8,128)}, u32[]{:S(2)}) copy-start(f32[2,2,256,256]{3,2,1,0:T(8,128)} %op_ref.1) | copy-start | bytes 3145732
  1.9 0.9 %copy-start.1 = (s32[3,8,1024]{2,1,0:T(8,128)S(1)}, s32[3,8,1024]{2,1,0:T(8,128)}, u32[]{:S(2)}) copy-start(s32[3,8,1024]{2,1,0:T(8,128)} %param.9) | copy-start | bytes 294916
  2.7 0.8 copy-start.2

commit v5 on v4

--- a/solution.py
+++ b/solution.py
@@ -320,7 +320,7 @@
             for copy in messages(o):
                 copy.start()
 
-        late = 1 if k == 0 else 0
+        late = 0
 
         def step(i, carry):
             far = at_chip(offset(i), 1 - core)
@@ -331,14 +331,11 @@
             sib_send[k, i, upper] = re
             sib_send[k, i, lower] = im
             if k == 0:
-                @pl.when(i == 1)
+                @pl.when(i == 0)
                 def _():
                     pl.semaphore_wait(barrier, jnp.where(own_part, 13, 14))
-                    swap(0).start()
-
-                @pl.when(i >= 1)
-                def _():
-                    swap(i).start()
+
+                swap(i).start()
 
                 @pl.when(i == 3)
                 def _():

time: 83.3 us -> 81.8 us (0.982)
  Pallas kernels: 79.4 us -> 77.9 us
    pallas_call x1, Pallas kernels: 64.7 us -> 63.2 us  [per_device(): pl.pallas_call(window_kernel, out_shape=(jax.ShapeDtypeStruct((LANES, WID...]
where the time goes in v5:
time: 81.8 us; the launch traced here: 81.5 us
  Pallas kernels  77.9 us (95%)
  local copies, waits for them, and re-layouts  2.87 us (4%)
  between operations  0.82 us (1%)
    pallas_call x1, Pallas kernels, per_device(): pl.pallas_call(window_kernel, out_shape=(jax.ShapeDtypeStruct((LANES, WID...  63.2 us
    pallas_call x1, Pallas kernels, per_device(): pl.pallas_call(final_kernel, out_shape=(jax.ShapeDtypeStruct((NBLK, 1, LA...  9.31 us
    pallas_call x1, Pallas kernels, prepare(): pl.pallas_call(prepare_kernel, out_shape=(jax.ShapeDtypeStruct((2 * WIDE,...  5.37 us
    unnamed x6, local copies, waits for them, and re-layouts  2.87 us

profile of v5, /device:TPU:1, one launch (start us, length us, event | category | flops | bytes accessed | tf_op | source)
XLA Modules:
  0.0 81.5 jit_solution(16109905893302980966)
XLA Ops:
  0.6 0.0 copy-start
  0.6 1.2 %copy-done = f32[2,2,256,256]{3,2,1,0:T(8,128)S(1)} copy-done((f32[2,2,256,256]{3,2,1,0:T(8,128)S(1)}, f32[2,2,256,256]{3,2,1,0:T(8,128)}, u32[]{:S(2)}) %copy-start) | copy-done | bytes 1048600
  1.9 0.0 copy-start.1
  1.9 0.9 %copy-done.1 = s32[3,8,1024]{2,1,0:T(8,128)S(1)} copy-done((s32[3,8,1024]{2,1,0:T(8,128)S(1)}, s32[3,8,1024]{2,1,0:T(8,128)}, u32[]{:S(2)}) %copy-start.1) | copy-done | bytes 98328
  2.7 0.0 copy-start.2
  2.8 0.8 copy-done.2
  3.5 5.4 %shard_map.68 = (bf16[1024,256]{1,0:T(8,128)(2,1)S(1)}, s32[8,24,8,128]{3,2,1,0:T(8,128)S(1)}, f32[8,8,8,128]{3,2,1,0:T(8,128)S(1)}) custom-call(f32[2,2,256,256]{3,2,1,0:T(8,128)S(1)} %copy-done, s32[24,1024]{1,0:T(8,128)S(1)} %bitcast.1, f32[8,1024]{1,0:T(8,128)S(1)} %copy-done.2), custom_call_target="tpu_custom_call" | custom-call | tf_op jit(solution)/shard_map/pallas_call | solution.py:82
  8.9 63.2 %shard_map.69 = (f32[128,512]{1,0:T(8,128)S(1)}, bf16[128,512]{1,0:T(8,128)(2,1)S(1)}, f32[512,128]{1,0:T(8,128)S(1)}) custom-call(bf16[2,2048,1024]{2,1,0:T(8,128)(2,1)} %green_hbm.1, bf16[2048,512]{1,0:T(8,128)(2,1)} %panel_hbm.1, bf16[1024,256]{1,0:T(8,128)(2,1)S(1)} %get-tuple-element.8.inv_in, s32[8,24,8,128]{3,2,1,0:T(8,128)S(1)} %get-tuple-element.9.pair_wide, ...), custom_call_target="tpu_custom_call" | custom-call | tf_op jit(solution)/shard_map/pallas_call | solution.py:552
  72.1 9.3 %shard_map.70 = (f32[2,1,128,512]{3,2,1,0:T(8,128)}, bf16[2,1,128,512]{3,2,1,0:T(8,128)(2,1)}) custom-call(f32[128,512]{1,0:T(8,128)S(1)} %get-tuple-element.11.rows_first, bf16[128,512]{1,0:T(8,128)(2,1)S(1)} %get-tuple-element.12.sigma_first, f32[512,128]{1,0:T(8,128)S(1)} %get-tuple-element.13.held, s32[8,24,8,128]{3,2,1,0:T(8,128)S(1)} %get-tuple-element.9.pair_wide, ...), custom_call_target="tpu_custom_call" | custom-call | tf_op jit(solution)/shard_map/pallas_call | solution.py:588
Async XLA Ops:
  0.6 1.2 %copy-start = (f32[2,2,256,256]{3,2,1,0:T(8,128)S(1)}, f32[2,2,256,256]{3,2,1,0:T(8,128)}, u32[]{:S(2)}) copy-start(f32[2,2,256,256]{3,2,1,0:T(8,128)} %op_ref.1) | copy-start | bytes 3145732
  1.9 0.9 %copy-start.1 = (s32[3,8,1024]{2,1,0:T(8,128)S(1)}, s32[3,8,1024]{2,1,0:T(8,128)}, u32[]{:S(2)}) copy-start(s32[3,8,1024]{2,1,0:T(8,128)} %param.9) | copy-start | bytes 294916
  2.7 0.8 copy-start.2

commit v6 on v5

--- a/solution.py
+++ b/solution.py
@@ -516,11 +516,10 @@
     tiles(0, 4)
     collect(0, True)
     exchange(0)
-    tiles(4, 6)
-    relay_first(0)
-    tiles(6, 8)
+    tiles(4, 8)
     collect(1, True)
     exchange(1)
+    relay_first(0)
     relay_second(0)
     rows_ref[...] = held[...].T
     sigma_ref[...] = sig[...].T.astype(bf16)

time: 81.8 us -> 82.4 us (level)
  no operation moved by 1% of the time
where the time goes in v6:
time: 82.4 us; the launch traced here: 82.2 us
  Pallas kernels  78.5 us (95%)
  local copies, waits for them, and re-layouts  2.87 us (3%)
    pallas_call x1, Pallas kernels, per_device(): pl.pallas_call(window_kernel, out_shape=(jax.ShapeDtypeStruct((LANES, WID...  63.8 us
    pallas_call x1, Pallas kernels, per_device(): pl.pallas_call(final_kernel, out_shape=(jax.ShapeDtypeStruct((NBLK, 1, LA...  9.31 us
    pallas_call x1, Pallas kernels, prepare(): pl.pallas_call(prepare_kernel, out_shape=(jax.ShapeDtypeStruct((2 * WIDE,...  5.37 us
    unnamed x6, local copies, waits for them, and re-layouts  2.87 us

profile of v6, /device:TPU:1, one launch (start us, length us, event | category | flops | bytes accessed | tf_op | source)
XLA Modules:
  0.0 82.2 jit_solution(16750753219822312348)
XLA Ops:
  0.6 0.0 copy-start
  0.6 1.2 %copy-done = f32[2,2,256,256]{3,2,1,0:T(8,128)S(1)} copy-done((f32[2,2,256,256]{3,2,1,0:T(8,128)S(1)}, f32[2,2,256,256]{3,2,1,0:T(8,128)}, u32[]{:S(2)}) %copy-start) | copy-done | bytes 1048600
  1.9 0.0 copy-start.1
  1.9 0.9 %copy-done.1 = s32[3,8,1024]{2,1,0:T(8,128)S(1)} copy-done((s32[3,8,1024]{2,1,0:T(8,128)S(1)}, s32[3,8,1024]{2,1,0:T(8,128)}, u32[]{:S(2)}) %copy-start.1) | copy-done | bytes 98328
  2.7 0.0 copy-start.2
  2.8 0.8 copy-done.2
  3.5 5.4 %shard_map.68 = (bf16[1024,256]{1,0:T(8,128)(2,1)S(1)}, s32[8,24,8,128]{3,2,1,0:T(8,128)S(1)}, f32[8,8,8,128]{3,2,1,0:T(8,128)S(1)}) custom-call(f32[2,2,256,256]{3,2,1,0:T(8,128)S(1)} %copy-done, s32[24,1024]{1,0:T(8,128)S(1)} %bitcast.1, f32[8,1024]{1,0:T(8,128)S(1)} %copy-done.2), custom_call_target="tpu_custom_call" | custom-call | tf_op jit(solution)/shard_map/pallas_call | solution.py:82
  8.9 63.8 %shard_map.69 = (f32[128,512]{1,0:T(8,128)S(1)}, bf16[128,512]{1,0:T(8,128)(2,1)S(1)}, f32[512,128]{1,0:T(8,128)S(1)}) custom-call(bf16[2,2048,1024]{2,1,0:T(8,128)(2,1)} %green_hbm.1, bf16[2048,512]{1,0:T(8,128)(2,1)} %panel_hbm.1, bf16[1024,256]{1,0:T(8,128)(2,1)S(1)} %get-tuple-element.8.inv_in, s32[8,24,8,128]{3,2,1,0:T(8,128)S(1)} %get-tuple-element.9.pair_wide, ...), custom_call_target="tpu_custom_call" | custom-call | tf_op jit(solution)/shard_map/pallas_call | solution.py:551
  72.7 9.3 %shard_map.70 = (f32[2,1,128,512]{3,2,1,0:T(8,128)}, bf16[2,1,128,512]{3,2,1,0:T(8,128)(2,1)}) custom-call(f32[128,512]{1,0:T(8,128)S(1)} %get-tuple-element.11.rows_first, bf16[128,512]{1,0:T(8,128)(2,1)S(1)} %get-tuple-element.12.sigma_first, f32[512,128]{1,0:T(8,128)S(1)} %get-tuple-element.13.held, s32[8,24,8,128]{3,2,1,0:T(8,128)S(1)} %get-tuple-element.9.pair_wide, ...), custom_call_target="tpu_custom_call" | custom-call | tf_op jit(solution)/shard_map/pallas_call | solution.py:587
Async XLA Ops:
  0.6 1.2 %copy-start = (f32[2,2,256,256]{3,2,1,0:T(8,128)S(1)}, f32[2,2,256,256]{3,2,1,0:T(8,128)}, u32[]{:S(2)}) copy-start(f32[2,2,256,256]{3,2,1,0:T(8,128)} %op_ref.1) | copy-start | bytes 3145732
  1.9 0.9 %copy-start.1 = (s32[3,8,1024]{2,1,0:T(8,128)S(1)}, s32[3,8,1024]{2,1,0:T(8,128)}, u32[]{:S(2)}) copy-start(s32[3,8,1024]{2,1,0:T(8,128)} %param.9) | copy-start | bytes 294916
  2.7 0.8 copy-start.2
